TPU v7x, 32 devices: a whole 2x2x4 slice. The times are simulated.
32 devices in a mesh: lat: 4 (over y, core), lon: 8 (over z, x).
Axes of the slice: x: 2, y: 2, z: 4, core: 2. Of those that a mesh axis runs over, the one named last changes fastest.
Arguments:
- field: bfloat16 [64, 128, 384], P('lat', 'lon'), may hold values from -6 to 6
- obs_jac: bfloat16 [32, 32, 128, 384], P(None, ('lat', 'lon')), may hold values from -0.3125 to 0.3125
- obs_frac: bfloat16 [32, 32, 2, 128], P(None, ('lat', 'lon')), may hold values from 0 to 1
- obs_innov: bfloat16 [32, 32, 128], P(None, ('lat', 'lon')), may hold values from -6 to 6
- obs_rinv: bfloat16 [32, 32, 128], P(None, ('lat', 'lon')), may hold values from 1 to 16
- obs_cells: int32 [32, 32, 128], P(None, ('lat', 'lon')), may hold values from -1 to 270, as said below
Outputs:
- departures: float32 [32, 32, 128], P(None, ('lat', 'lon'))
- field_grad: float32 [64, 128, 384], P('lat', 'lon')
Inputs may be any that keep to these rules, and one draw needn't show every extreme that they name: `obs_cells`: in block (o, p) the live slots come first, at least one and at most 128; a live slot holds r * 17 + q with r below 16 and q below 16; slot 0 of every block holds the cell at r = 15, q = 15; the number of live slots varies by owner.
All inputs are finite; a program needn't handle non-finite values.
Results may differ from a plain program's by a relative error of at most 0.0046.
Values may be sent and summed in bfloat16 or wider, within the bound.
A program may use at most 128 MiB of HBM per device.

v0:
```python
import functools
import math

import jax
import jax.numpy as jnp
from jax import lax
from jax.experimental import pallas as pl
from jax.experimental.pallas import tpu as pltpu
from jax.sharding import PartitionSpec as P

MESH = pl.DeviceIdType.MESH
AWAY = -1000.0


def weight_rows(position, frac, rows):
    ids = lax.broadcasted_iota(jnp.int32, (rows, position.shape[1]), 0).astype(jnp.float32)
    zero = jnp.zeros_like(ids)
    return jnp.where(
        ids == position, 1.0 - frac, jnp.where(ids == position + 1.0, frac, zero)
    )


def kernel(
    lat_n, lon_n, line, rows, cols, tile,
    field, cell_ref, frac_ref, innov_ref, rinv_ref, jac,
    grad, grecv, hrecv, dep_out,
    edge, innov, rinv, meta,
    tbl, met, jrecv, dep, gsend,
    t_send, t_recv, m_send, m_recv, j_send, j_recv, d_send, d_recv,
    g_send, g_recv, h_send, h_recv, from_low, from_high,
):
    inner = lon_n // line
    plane = lat_n * inner
    total = lat_n * lon_n
    slots = jac.shape[3]
    cells = rows * cols
    halo = cells + cols
    lat, lon = lax.axis_index("lat"), lax.axis_index("lon")
    z, xi = lon // inner, lon % inner
    here = lat * inner + xi
    lat_up, lat_down = (lat + 1) % lat_n, (lat + lat_n - 1) % lat_n
    lon_down = (lon + lon_n - 1) % lon_n
    z_low, x_low = lon_down // inner, lon_down % inner

    def remote(src, dst, send, recv, to):
        return pltpu.make_async_remote_copy(
            src_ref=src, dst_ref=dst, send_sem=send, recv_sem=recv,
            device_id=to, device_id_type=MESH,
        )

    def landed(like, sem):
        pltpu.make_async_copy(like, like, sem).wait()

    has_low, has_high = z > 0, z < line - 1
    low, high = (lat, lon - inner), (lat, lon + inner)
    barrier = pltpu.get_barrier_semaphore()

    @pl.when(has_low)
    def _():
        pl.semaphore_signal(barrier, inc=1, device_id=low, device_id_type=MESH)

    @pl.when(has_high)
    def _():
        pl.semaphore_signal(barrier, inc=1, device_id=high, device_id_type=MESH)

    def greet(i, carry):
        to = (here + i) % plane
        pl.semaphore_signal(
            barrier, inc=1, device_id=(to // inner, z * inner + to % inner), device_id_type=MESH
        )
        return carry

    lax.fori_loop(1, plane, greet, 0)

    mine = pl.ds(here * slots, slots)
    pltpu.make_async_copy(field, tbl.at[z, pl.ds(0, cells)], t_recv.at[z]).start()
    for n in range(line):
        g = (z + 1 + n) % line
        pltpu.make_async_copy(jac.at[lat, g, xi], jrecv.at[g, mine], j_recv.at[g]).start()
    pl.semaphore_wait(barrier, plane - 1 + has_low.astype(jnp.int32) + has_high.astype(jnp.int32))

    def send_jac(g):
        def one(i, carry):
            to = (here + i) % plane
            remote(
                jac.at[to // inner, g, to % inner], jrecv.at[g, mine], j_send, j_recv.at[g],
                (to // inner, z * inner + to % inner),
            ).start()
            return carry

        lax.fori_loop(1, plane, one, 0)

    def send_meta(i, carry):
        to = (here + i) % plane
        remote(
            meta.at[to], met.at[:, :, mine], m_send, m_recv,
            (to // inner, z * inner + to % inner),
        ).start()
        return carry

    send_jac((z + 1) % line)
    edge[...] = jnp.concatenate(
        [field[pl.ds(r * cols, cols), :].astype(jnp.float32)[0:1] for r in range(rows)], axis=0
    ).astype(edge.dtype)

    for _ in range(line - 1):
        @pl.when(has_low)
        def _():
            pl.semaphore_signal(from_high, inc=1, device_id=low, device_id_type=MESH)

        @pl.when(has_high)
        def _():
            pl.semaphore_signal(from_low, inc=1, device_id=high, device_id_type=MESH)

        @pl.when(has_low)
        def _():
            pl.semaphore_wait(from_low, 1)

        @pl.when(has_high)
        def _():
            pl.semaphore_wait(from_high, 1)

    for i in (*range(1, line), 0):
        to = (z + i) % line
        if i > 0:
            remote(field, tbl.at[z, pl.ds(0, cells)], t_send.at[0], t_recv.at[z],
                   (lat, to * inner + xi)).start()
        remote(field.at[pl.ds(0, cols)], tbl.at[z, pl.ds(cells, cols)], t_send.at[1],
               t_recv.at[z], (lat_down, to * inner + xi)).start()
        remote(edge, tbl.at[z_low, pl.ds(halo, rows)], t_send.at[1], t_recv.at[z_low],
               (lat, to * inner + x_low)).start()
        remote(edge, tbl.at[z_low, pl.ds(halo + rows, rows)], t_send.at[1], t_recv.at[z_low],
               (lat_down, to * inner + x_low)).start()
    send_jac((z + 2) % line)
    innov[...] = innov_ref[...].astype(jnp.float32)
    rinv[...] = rinv_ref[...].astype(jnp.float32)

    def build(k, carry):
        for g in range(line):
            owner = (k // inner) * lon_n + g * inner + k % inner
            cell = cell_ref[owner].astype(jnp.float32)
            live = cell >= 0.0
            row = jnp.floor((cell + 0.5) * (1.0 / (cols + 1)))
            meta[k, g] = jnp.concatenate(
                [
                    jnp.where(live, row, AWAY),
                    jnp.where(live, cell - row * (cols + 1), AWAY),
                    frac_ref[owner].astype(jnp.float32),
                    innov[pl.ds(owner, 1), :],
                    rinv[pl.ds(owner, 1), :],
                    jnp.zeros((2, slots), jnp.float32),
                ],
                axis=0,
            ).astype(meta.dtype)
        return carry

    lax.fori_loop(0, plane, build, 0)
    pltpu.make_async_copy(meta.at[here], met.at[:, :, mine], m_recv).start()

    lax.fori_loop(1, plane, send_meta, 0)
    for n in range(2, line):
        send_jac((z + 1 + n) % line)

    landed(met, m_recv)
    inside = jnp.where(lat < lat_n - 1, 1.0, 0.0)
    width = tile * slots
    tiles = plane // tile
    pad = -(-(max(rows, cols) + 1) // 8) * 8

    def group(n, carry):
        g = (z + 1 + n) % line
        landed(tbl.at[g], t_recv.at[g])
        landed(jrecv.at[g], j_recv.at[g])
        if tiles > 1:
            grad[...] = jnp.zeros_like(grad)

        def one_tile(t, inner_carry):
            lanes = pl.ds(pl.multiple_of(t * width, width), width)
            info = met[g, :, lanes].astype(jnp.float32)
            lat_w = weight_rows(info[0:1], info[2:3], pad)
            lon_w = weight_rows(info[1:2], info[3:4], pad)
            lon_c = lon_w[:cols]
            lon_e = lon_w[cols:cols + 1]
            lat_n_row = lat_w[rows:rows + 1] * inside
            first = lax.broadcasted_iota(jnp.int32, (rows, width), 0) == 0
            blocks = [lat_w[r:r + 1] * lon_c for r in range(rows)]
            blocks.append(lat_n_row * lon_c)
            blocks.append(lat_w[:rows] * lon_e)
            blocks.append(
                jnp.where(first, jnp.broadcast_to(lat_n_row * lon_e, (rows, width)), 0.0)
            )
            spread = jnp.concatenate(blocks, axis=0).astype(jnp.bfloat16).astype(jnp.float32)
            jac_t = jrecv[g, lanes]
            products = lax.dot_general(
                tbl[g], jac_t, (((1,), (1,)), ((), ())), preferred_element_type=jnp.float32
            )
            evolved = jnp.sum(spread * products, axis=0, keepdims=True)
            departure = jnp.where(info[0:1] >= 0.0, evolved - info[4:5], 0.0)
            dep[g, :, lanes] = departure
            scaled = (spread * (info[5:6] * departure)).astype(jnp.bfloat16)
            partial = jnp.dot(scaled, jac_t, preferred_element_type=jnp.float32)
            if tiles > 1:
                grad[...] += partial
            else:
                grad[...] = partial
            return inner_carry

        if tiles > 1:
            lax.fori_loop(0, tiles, one_tile, 0)
        else:
            one_tile(0, 0)
        gsend[g] = grad[...].astype(jnp.bfloat16)
        east = (g * inner + xi + 1) % lon_n
        remote(gsend.at[g, pl.ds(cells, cols)], hrecv.at[0, z], h_send, h_recv,
               (lat_up, g * inner + xi)).start()
        remote(gsend.at[g, pl.ds(halo, rows)], hrecv.at[1, z], h_send, h_recv,
               (lat, east)).start()
        remote(gsend.at[g, pl.ds(halo + rows, rows)], hrecv.at[2, z], h_send, h_recv,
               (lat_up, east)).start()

        @pl.when(n < line - 1)
        def _():
            slot = lax.rem(n, line - 1)
            remote(gsend.at[g, pl.ds(0, cells)], grecv.at[slot], g_send, g_recv,
                   (lat, g * inner + xi)).start()

        def send_dep(i, inner_carry):
            to = (here + i) % plane
            remote(
                dep.at[g, :, pl.ds(to * slots, slots)], dep_out.at[lat, g, xi], d_send, d_recv,
                (to // inner, z * inner + to % inner),
            ).start()
            return inner_carry

        lax.fori_loop(1, plane, send_dep, 0)
        pltpu.make_async_copy(dep.at[g, :, mine], dep_out.at[lat, g, xi], d_recv).start()
        return carry

    lax.fori_loop(0, line, group, 0)

    others = pl.ds(0, (plane - 1) * slots)
    landed(grecv, g_recv)
    landed(hrecv, h_recv)
    landed(dep_out, d_recv)
    landed(grecv, t_send.at[0])
    landed(tbl.at[:, pl.ds(cells, cols + 2 * rows)], t_send.at[1])
    landed(met.at[:, :, others], m_send)
    landed(jrecv.at[:, others], j_send)
    landed(dep.at[:, :, others], d_send)
    landed(grecv, g_send)
    landed(gsend.at[:, pl.ds(cells, cols + 2 * rows)], h_send)


def last_sums(rows, cols, grad, grecv, hrecv, dep, grad_out, dep_out):
    dep_out[...] = dep[...]
    field_sum = grad[pl.ds(0, rows * cols), :]
    for slot in range(grecv.shape[0]):
        field_sum = field_sum + grecv[slot].astype(jnp.float32)
    grad_out[...] = field_sum
    grad_out[pl.ds(0, cols), :] += jnp.sum(hrecv[0].astype(jnp.float32), axis=0)
    east_sum = jnp.sum(hrecv[1].astype(jnp.float32), axis=0)
    corner_sum = jnp.sum(hrecv[2].astype(jnp.float32), axis=0)
    for r in range(rows):
        extra = east_sum[r:r + 1]
        if r == 0:
            extra = extra + corner_sum[0:1]
        grad_out[pl.ds(r * cols, 1), :] += extra


def shards(mesh_shape, field, obs_jac, obs_frac, obs_innov, obs_rinv, obs_cells):
    lat_n, lon_n = mesh_shape
    line = math.gcd(lon_n // 2, 4)
    inner = lon_n // line
    plane = lat_n * inner
    total = lat_n * lon_n
    rows, cols, wide = field.shape
    slots = obs_jac.shape[2]
    tile = math.gcd(plane, 8)
    cells = rows * cols
    table = cells + cols + 2 * rows
    f32, bf16 = jnp.float32, jnp.bfloat16
    dma = pltpu.SemaphoreType.DMA
    one = pltpu.SemaphoreType.DMA(())
    vmem = pl.BlockSpec(memory_space=pltpu.VMEM)
    parts = pl.pallas_call(
        functools.partial(kernel, lat_n, lon_n, line, rows, cols, tile),
        out_shape=(
            jax.ShapeDtypeStruct((table, wide), f32),
            jax.ShapeDtypeStruct((line - 1, cells, wide), bf16),
            jax.ShapeDtypeStruct((3, line, rows, wide), bf16),
            jax.ShapeDtypeStruct((lat_n, line, inner, 1, slots), f32),
        ),
        in_specs=[vmem, vmem, vmem, vmem, vmem, pl.BlockSpec(memory_space=pl.ANY)],
        out_specs=(vmem,) * 4,
        scratch_shapes=[
            pltpu.VMEM((rows, wide), bf16),
            pltpu.VMEM((total, slots), f32),
            pltpu.VMEM((total, slots), f32),
            pltpu.VMEM((plane, line, 8, slots), bf16),
            pltpu.VMEM((line, table, wide), bf16),
            pltpu.VMEM((line, 8, plane * slots), bf16),
            pltpu.VMEM((line, plane * slots, wide), bf16),
            pltpu.VMEM((line, 1, plane * slots), f32),
            pltpu.VMEM((line, table, wide), bf16),
            dma((2,)), dma((line,)),
            one, one,
            one, dma((line,)),
            one, one,
            one, one,
            one, one,
            pltpu.SemaphoreType.REGULAR, pltpu.SemaphoreType.REGULAR,
        ],
        compiler_params=pltpu.CompilerParams(
            collective_id=0, has_side_effects=True, vmem_limit_bytes=60 * 1024 * 1024
        ),
    )(
        field.reshape(cells, wide),
        obs_cells,
        obs_frac.reshape(total, 2, slots),
        obs_innov.reshape(total, slots),
        obs_rinv.reshape(total, slots),
        obs_jac.reshape(lat_n, line, inner, slots, wide),
    )
    grad, departures = pl.pallas_call(
        functools.partial(last_sums, rows, cols),
        out_shape=(
            jax.ShapeDtypeStruct((cells, wide), f32),
            jax.ShapeDtypeStruct((total, 1, slots), f32),
        ),
        in_specs=[vmem] * 4,
        out_specs=(vmem, vmem),
    )(*parts[:3], parts[3].reshape(total, 1, slots))
    return departures, grad.reshape(rows, cols, wide)


def solution(mesh):
    placed = (
        P("lat", "lon", None),
        P(None, ("lat", "lon"), None, None),
        P(None, ("lat", "lon"), None, None),
        P(None, ("lat", "lon"), None),
        P(None, ("lat", "lon"), None),
        P(None, ("lat", "lon"), None),
    )
    return jax.shard_map(
        functools.partial(shards, (mesh.shape["lat"], mesh.shape["lon"])),
        mesh=mesh,
        in_specs=placed,
        out_specs=(P(None, ("lat", "lon"), None), P("lat", "lon", None)),
        check_vma=False,
    )
```

profile of v0, /device:TPU:0, one launch (start us, length us, event | category | flops | bytes accessed | tf_op | source)
XLA Modules:
  0.0 55.6 jit_solution(4337480725784569001)
XLA Ops:
  0.6 52.8 %shard_map.77 = (f32[304,384]{1,0:T(8,128)}, bf16[3,256,384]{2,1,0:T(8,128)(2,1)}, bf16[3,4,16,384]{3,2,1,0:T(8,128)(2,1)}, f32[4,4,2,1,128]{4,3,2,1,0:T(1,128)}) custom-call(bf16[256,384]{1,0:T(8,128)(2,1)} %bitcast.8, s32[32,1,128]{2,1,0:T(1,128)} %cell_ref.1, bf16[32,2,128]{2,1,0:T(2,128)(2,1)} %bitcast.9, bf16[32,128]{1,0:T(8,128)(2,1)} %bitcast.11, ...), custom_call_target="tpu_custom_call" | custom-call | tf_op jit(solution)/shard_map/pallas_call | solution.py:285
  53.4 2.1 %shard_map.78 = (f32[256,384]{1,0:T(8,128)}, f32[32,1,128]{2,1,0:T(1,128)}) custom-call(f32[304,384]{1,0:T(8,128)} %get-tuple-element.8.grad, bf16[3,256,384]{2,1,0:T(8,128)(2,1)} %get-tuple-element.9.grecv, bf16[3,4,16,384]{3,2,1,0:T(8,128)(2,1)} %get-tuple-element.10.hrecv, f32[32,1,128]{2,1,0:T(1,128)} %bitcast.10), custom_call_target="tpu_custom_call" | custom-call | tf_op jit(solution)/shard_map/pallas_call | solution.py:324
where the time goes:
time: 55.7 us; the launch traced here: 55.6 us
  Pallas kernels  54.9 us (99%)
  between operations  0.64 us (1%)
    pallas_call x1, Pallas kernels, shards(): pl.pallas_call(functools.partial(kernel, lat_n, lon_n, line, rows, cols,...  52.8 us
    pallas_call x1, Pallas kernels, shards(): pl.pallas_call(functools.partial(last_sums, rows, cols), out_shape=(jax.S...  2.12 us

commit v1 on v0

v1 whole, which is shorter than its diff:
```python
import functools
import math

import jax
import jax.numpy as jnp
from jax import lax
from jax.experimental import pallas as pl
from jax.experimental.pallas import tpu as pltpu
from jax.sharding import PartitionSpec as P

MESH = pl.DeviceIdType.MESH
AWAY = -1000.0


def visit_order(z, line):
    half = line // 2
    if z < half:
        return [*range(half, line), *(p for p in range(half) if p != z), z]
    return [*range(half - 1, -1, -1), *(p for p in range(half, line) if p != z), z]


def pick(z, values):
    chosen = jnp.int32(values[0])
    for p in range(1, len(values)):
        chosen = jnp.where(z == p, jnp.int32(values[p]), chosen)
    return chosen


def weight_rows(position, frac, rows):
    ids = lax.broadcasted_iota(jnp.int32, (rows, position.shape[1]), 0).astype(jnp.float32)
    zero = jnp.zeros_like(ids)
    return jnp.where(
        ids == position, 1.0 - frac, jnp.where(ids == position + 1.0, frac, zero)
    )


def kernel(
    lat_n, lon_n, line, rows, cols, tile,
    field, cell_ref, frac_ref, innov_ref, rinv_ref, jac,
    gmain, hrecv, dep_out,
    edge, innov, rinv, meta,
    tbl, met, jrecv, dep, part, gsend, rbuf, hsend,
    f_send, f_recv, e_send, e_recv, m_send, m_recv, j_send, j_recv, d_send, d_recv,
    g_send, g_recv, h_send, h_recv, from_low, from_high,
):
    inner = lon_n // line
    plane = lat_n * inner
    slots = jac.shape[3]
    cells = rows * cols
    halo = cells + cols
    lat, lon = lax.axis_index("lat"), lax.axis_index("lon")
    z, xi = lon // inner, lon % inner
    here = lat * inner + xi
    lat_up, lat_down = (lat + 1) % lat_n, (lat + lat_n - 1) % lat_n
    lon_up, lon_down = (lon + 1) % lon_n, (lon + lon_n - 1) % lon_n
    z_low, x_low = lon_down // inner, lon_down % inner
    orders = [visit_order(p, line) for p in range(line)]
    visits = [pick(z, [order[n] for order in orders]) for n in range(line)]

    def remote(src, dst, send, recv, to):
        return pltpu.make_async_remote_copy(
            src_ref=src, dst_ref=dst, send_sem=send, recv_sem=recv,
            device_id=to, device_id_type=MESH,
        )

    def landed(like, sem):
        pltpu.make_async_copy(like, like, sem).wait()

    def mate(i):
        to = (here + i) % plane
        return to, (to // inner, z * inner + to % inner)

    has_low, has_high = z > 0, z < line - 1
    inside_line = has_low & has_high
    low, high = (lat, lon - inner), (lat, lon + inner)
    barrier = pltpu.get_barrier_semaphore()

    @pl.when(has_low)
    def _():
        pl.semaphore_signal(barrier, inc=1, device_id=low, device_id_type=MESH)

    @pl.when(has_high)
    def _():
        pl.semaphore_signal(barrier, inc=1, device_id=high, device_id_type=MESH)

    def greet(i, carry):
        pl.semaphore_signal(barrier, inc=1, device_id=mate(i)[1], device_id_type=MESH)
        return carry

    lax.fori_loop(1, plane, greet, 0)

    own_field = tbl.at[z, pl.ds(0, cells)]
    pltpu.make_async_copy(field, own_field, f_recv.at[z]).start()
    for g in visits:
        pltpu.make_async_copy(
            jac.at[lat, g, xi], jrecv.at[g, pl.ds(0, slots)], j_recv.at[g]
        ).start()
    innov[...] = innov_ref[...].astype(jnp.float32)
    rinv[...] = rinv_ref[...].astype(jnp.float32)

    def build(i, carry):
        to, _ = mate(i)
        for g in range(line):
            owner = (to // inner) * lon_n + g * inner + to % inner
            cell = cell_ref[owner].astype(jnp.float32)
            live = cell >= 0.0
            row = jnp.floor((cell + 0.5) * (1.0 / (cols + 1)))
            meta[i, g] = jnp.concatenate(
                [
                    jnp.where(live, row, AWAY),
                    jnp.where(live, cell - row * (cols + 1), AWAY),
                    frac_ref[owner].astype(jnp.float32),
                    innov[pl.ds(owner, 1), :],
                    rinv[pl.ds(owner, 1), :],
                    jnp.zeros((2, slots), jnp.float32),
                ],
                axis=0,
            ).astype(meta.dtype)
        return carry

    lax.fori_loop(0, plane, build, 0)
    landed(own_field, f_recv.at[z])
    edge[...] = jnp.concatenate(
        [tbl[z, pl.ds(r * cols, cols), :].astype(jnp.float32)[0:1] for r in range(rows)], axis=0
    ).astype(edge.dtype)
    pltpu.make_async_copy(meta.at[0], met.at[:, :, pl.ds(0, slots)], m_recv).start()
    pl.semaphore_wait(barrier, plane - 1 + has_low.astype(jnp.int32) + has_high.astype(jnp.int32))

    def send_field(g, up):
        piece = tbl.at[g, pl.ds(0, cells)]
        remote(piece, piece, f_send, f_recv.at[g], high if up else low).start()

    @pl.when(has_low)
    def _():
        send_field(z, False)

    @pl.when(has_high)
    def _():
        send_field(z, True)

    def send_meta(i, carry):
        place = pl.ds(pl.multiple_of(i * slots, slots), slots)
        remote(meta.at[i], met.at[:, :, place], m_send, m_recv, mate(i)[1]).start()
        return carry

    def send_jac(n):
        g = visits[n]

        def one(i, carry):
            to, at = mate(i)
            place = pl.ds(pl.multiple_of(i * slots, slots), slots)
            remote(
                jac.at[to // inner, g, to % inner], jrecv.at[g, place], j_send, j_recv.at[g], at
            ).start()
            return carry

        return one

    lax.fori_loop(1, plane, send_meta, 0)
    lax.fori_loop(1, plane // 2, send_jac(0), 0)

    for _ in range(line - 1):
        @pl.when(has_low)
        def _():
            pl.semaphore_signal(from_high, inc=1, device_id=low, device_id_type=MESH)

        @pl.when(has_high)
        def _():
            pl.semaphore_signal(from_low, inc=1, device_id=high, device_id_type=MESH)

        @pl.when(has_low)
        def _():
            pl.semaphore_wait(from_low, 1)

        @pl.when(has_high)
        def _():
            pl.semaphore_wait(from_high, 1)

    for i in range(line):
        to = (z + i) % line
        remote(tbl.at[z, pl.ds(0, cols)], tbl.at[z, pl.ds(cells, cols)], e_send,
               e_recv.at[z], (lat_down, to * inner + xi)).start()
        remote(edge, tbl.at[z_low, pl.ds(halo, rows)], e_send,
               e_recv.at[z_low], (lat, to * inner + x_low)).start()
        remote(edge, tbl.at[z_low, pl.ds(halo + rows, rows)], e_send,
               e_recv.at[z_low], (lat_down, to * inner + x_low)).start()
    lax.fori_loop(plane // 2, plane, send_jac(0), 0)
    for n in range(1, line):
        lax.fori_loop(1, plane, send_jac(n), 0)

    def forward(d):
        @pl.when(inside_line & (z >= d))
        def _():
            landed(own_field, f_recv.at[z - d])
            send_field(z - d, True)

        @pl.when(inside_line & (z + d < line))
        def _():
            landed(own_field, f_recv.at[z + d])
            send_field(z + d, False)

    landed(met, m_recv)
    inside = jnp.where(lat < lat_n - 1, 1.0, 0.0)
    width = tile * slots
    tiles = plane // tile
    pad = -(-(max(rows, cols) + 1) // 8) * 8

    def compute(n, g):
        into = part.at[n]
        if tiles > 1:
            into[...] = jnp.zeros(into.shape, into.dtype)

        def one_tile(t, carry):
            lanes = pl.ds(pl.multiple_of(t * width, width), width)
            info = met[g, :, lanes].astype(jnp.float32)
            lat_w = weight_rows(info[0:1], info[2:3], pad)
            lon_w = weight_rows(info[1:2], info[3:4], pad)
            lon_c = lon_w[:cols]
            lon_e = lon_w[cols:cols + 1]
            lat_n_row = lat_w[rows:rows + 1] * inside
            first = lax.broadcasted_iota(jnp.int32, (rows, width), 0) == 0
            blocks = [lat_w[r:r + 1] * lon_c for r in range(rows)]
            blocks.append(lat_n_row * lon_c)
            blocks.append(lat_w[:rows] * lon_e)
            blocks.append(
                jnp.where(first, jnp.broadcast_to(lat_n_row * lon_e, (rows, width)), 0.0)
            )
            spread = jnp.concatenate(blocks, axis=0).astype(jnp.bfloat16).astype(jnp.float32)
            jac_t = jrecv[g, lanes]
            products = lax.dot_general(
                tbl[g], jac_t, (((1,), (1,)), ((), ())), preferred_element_type=jnp.float32
            )
            evolved = jnp.sum(spread * products, axis=0, keepdims=True)
            departure = jnp.where(info[0:1] >= 0.0, evolved - info[4:5], 0.0)
            dep[g, :, lanes] = departure
            scaled = (spread * (info[5:6] * departure)).astype(jnp.bfloat16)
            partial = jnp.dot(scaled, jac_t, preferred_element_type=jnp.float32)
            if tiles > 1:
                into[...] += partial
            else:
                into[...] = partial
            return carry

        if tiles > 1:
            lax.fori_loop(0, tiles, one_tile, 0)
        else:
            one_tile(0, 0)

    def send_dep(g):
        def one(i, carry):
            to = (here + plane - i) % plane
            place = pl.ds(pl.multiple_of(i * slots, slots), slots)
            remote(
                dep.at[g, :, place], dep_out.at[lat, g, xi], d_send, d_recv,
                (to // inner, z * inner + to % inner),
            ).start()
            return carry

        lax.fori_loop(1, plane, one, 0)
        pltpu.make_async_copy(dep.at[g, :, pl.ds(0, slots)], dep_out.at[lat, g, xi], d_recv).start()

    def finish(n, incoming):
        g = visits[n]
        total = part[n]
        if incoming:
            landed(rbuf.at[g], g_recv.at[g])
            total = total + rbuf[g].astype(jnp.float32)
        gsend[n] = total.astype(gsend.dtype)
        up = g > z
        next_z = jnp.where(up, z + 1, z - 1)
        slot = jnp.where((g == next_z) & jnp.logical_not(up), line, g)
        remote(gsend.at[n], rbuf.at[slot], g_send, g_recv.at[slot],
               (lat, next_z * inner + xi)).start()

    def pass_on(n):
        @pl.when(inside_line)
        def _():
            finish(n, True)

    for d in range(1, max(line // 2, 1)):
        forward(d)
    for n in range(line):
        g = visits[n]
        if n < line - 1:
            @pl.when(jnp.logical_not(inside_line))
            def _():
                landed(own_field, f_recv.at[g])
        landed(tbl.at[g, pl.ds(cells, cols + 2 * rows)], e_recv.at[g])
        landed(jrecv.at[g], j_recv.at[g])
        compute(n, g)
        send_dep(g)
        if n < line - 1:
            @pl.when(jnp.logical_not(inside_line))
            def _():
                finish(n, False)
        if n == 0:
            for d in range(max(line // 2, 1), line - 1):
                forward(d)
        elif n == 1 and n < line - 1:
            pass_on(0)
            pass_on(1)
        elif n < line - 1:
            pass_on(n)

    @pl.when(has_low)
    def _():
        landed(rbuf.at[z], g_recv.at[z])
        part[line - 1] += rbuf[z].astype(jnp.float32)

    @pl.when(has_high)
    def _():
        landed(rbuf.at[line], g_recv.at[line])
        part[line - 1] += rbuf[line].astype(jnp.float32)

    hsend[...] = part[line - 1, pl.ds(cells, cols + 2 * rows), :].astype(hsend.dtype)
    remote(hsend.at[pl.ds(0, cols)], hrecv.at[0], h_send, h_recv, (lat_up, lon)).start()
    remote(hsend.at[pl.ds(cols, rows)], hrecv.at[1], h_send, h_recv, (lat, lon_up)).start()
    remote(hsend.at[pl.ds(cols + rows, rows)], hrecv.at[2], h_send, h_recv,
           (lat_up, lon_up)).start()
    gmain[...] = part[line - 1, pl.ds(0, cells), :]

    others = pl.ds(0, (plane - 1) * slots)
    for up in (False, True):
        for i in range(line):
            sent = (z >= i) & has_high if up else (z + i < line) & has_low

            @pl.when(sent & (inside_line | (i == 0)))
            def _():
                landed(own_field, f_send)
    landed(tbl.at[:, pl.ds(cells, cols + 2 * rows)], e_send)
    landed(met.at[:, :, others], m_send)
    landed(jrecv.at[:, others], j_send)
    landed(dep.at[:, :, others], d_send)
    landed(gsend, g_send)
    landed(hsend, h_send)
    landed(hrecv, h_recv)
    landed(dep_out, d_recv)


def last_sums(rows, cols, gmain, hrecv, dep, grad_out, dep_out):
    dep_out[...] = dep[...]
    grad_out[...] = gmain[...]
    grad_out[pl.ds(0, cols), :] += hrecv[0].astype(jnp.float32)
    east = hrecv[1].astype(jnp.float32)
    corner = hrecv[2].astype(jnp.float32)
    for r in range(rows):
        extra = east[r:r + 1]
        if r == 0:
            extra = extra + corner[0:1]
        grad_out[pl.ds(r * cols, 1), :] += extra


def shards(mesh_shape, field, obs_jac, obs_frac, obs_innov, obs_rinv, obs_cells):
    lat_n, lon_n = mesh_shape
    line = math.gcd(lon_n // 2, 4)
    inner = lon_n // line
    plane = lat_n * inner
    total = lat_n * lon_n
    rows, cols, wide = field.shape
    slots = obs_jac.shape[2]
    tile = math.gcd(plane, 8)
    cells = rows * cols
    table = cells + cols + 2 * rows
    f32, bf16 = jnp.float32, jnp.bfloat16
    dma = pltpu.SemaphoreType.DMA
    one = pltpu.SemaphoreType.DMA(())
    vmem = pl.BlockSpec(memory_space=pltpu.VMEM)
    anywhere = pl.BlockSpec(memory_space=pl.ANY)
    parts = pl.pallas_call(
        functools.partial(kernel, lat_n, lon_n, line, rows, cols, tile),
        out_shape=(
            jax.ShapeDtypeStruct((cells, wide), f32),
            jax.ShapeDtypeStruct((3, rows, wide), bf16),
            jax.ShapeDtypeStruct((lat_n, line, inner, 1, slots), f32),
        ),
        in_specs=[anywhere, vmem, vmem, vmem, vmem, anywhere],
        out_specs=(vmem,) * 3,
        scratch_shapes=[
            pltpu.VMEM((rows, wide), bf16),
            pltpu.VMEM((total, slots), f32),
            pltpu.VMEM((total, slots), f32),
            pltpu.VMEM((plane, line, 8, slots), bf16),
            pltpu.VMEM((line, table, wide), bf16),
            pltpu.VMEM((line, 8, plane * slots), bf16),
            pltpu.VMEM((line, plane * slots, wide), bf16),
            pltpu.VMEM((line, 1, plane * slots), f32),
            pltpu.VMEM((line, table, wide), f32),
            pltpu.VMEM((line - 1, table, wide), bf16),
            pltpu.VMEM((line + 1, table, wide), bf16),
            pltpu.VMEM((table - cells, wide), bf16),
            one, dma((line,)),
            one, dma((line,)),
            one, one,
            one, dma((line,)),
            one, one,
            one, dma((line + 1,)),
            one, one,
            pltpu.SemaphoreType.REGULAR, pltpu.SemaphoreType.REGULAR,
        ],
        compiler_params=pltpu.CompilerParams(
            collective_id=0, has_side_effects=True, vmem_limit_bytes=60 * 1024 * 1024
        ),
    )(
        field.reshape(cells, wide),
        obs_cells,
        obs_frac.reshape(total, 2, slots),
        obs_innov.reshape(total, slots),
        obs_rinv.reshape(total, slots),
        obs_jac.reshape(lat_n, line, inner, slots, wide),
    )
    grad, departures = pl.pallas_call(
        functools.partial(last_sums, rows, cols),
        out_shape=(
            jax.ShapeDtypeStruct((cells, wide), f32),
            jax.ShapeDtypeStruct((total, 1, slots), f32),
        ),
        in_specs=[vmem] * 3,
        out_specs=(vmem, vmem),
    )(*parts[:2], parts[2].reshape(total, 1, slots))
    return departures, grad.reshape(rows, cols, wide)


def solution(mesh):
    placed = (
        P("lat", "lon", None),
        P(None, ("lat", "lon"), None, None),
        P(None, ("lat", "lon"), None, None),
        P(None, ("lat", "lon"), None),
        P(None, ("lat", "lon"), None),
        P(None, ("lat", "lon"), None),
    )
    return jax.shard_map(
        functools.partial(shards, (mesh.shape["lat"], mesh.shape["lon"])),
        mesh=mesh,
        in_specs=placed,
        out_specs=(P(None, ("lat", "lon"), None), P("lat", "lon", None)),
        check_vma=False,
    )
```

time: 55.7 us -> 55.4 us (level)
  the two profiles are of different devices: /device:TPU:0 before, /device:TPU:9 now
where the time goes in v1:
time: 55.4 us; the launch traced here: 55.1 us
  Pallas kernels  54.5 us (98%)
  between operations  0.64 us (1%)
    pallas_call x1, Pallas kernels, shards(): pl.pallas_call(functools.partial(kernel, lat_n, lon_n, line, rows, cols,...  52.7 us
    pallas_call x1, Pallas kernels, shards(): pl.pallas_call(functools.partial(last_sums, rows, cols), out_shape=(jax.S...  1.81 us

profile of v1, /device:TPU:9, one launch (start us, length us, event | category | flops | bytes accessed | tf_op | source)
XLA Modules:
  0.0 55.1 jit_solution(2432314397939850374)
XLA Ops:
  0.6 52.7 %shard_map.77 = (f32[256,384]{1,0:T(8,128)}, bf16[3,16,384]{2,1,0:T(8,128)(2,1)}, f32[4,4,2,1,128]{4,3,2,1,0:T(1,128)}) custom-call(bf16[256,384]{1,0:T(8,128)(2,1)} %bitcast.8, s32[32,1,128]{2,1,0:T(1,128)} %cell_ref.1, bf16[32,2,128]{2,1,0:T(2,128)(2,1)} %bitcast.9, bf16[32,128]{1,0:T(8,128)(2,1)} %bitcast.11, bf16[32,128]{1,0:T(8,128)(2,1)} %bitcast.12, ...), custom_call_target="tpu_custom_call" | custom-call | tf_op jit(solution)/shard_map/pallas_call | solution.py:369
  53.3 1.8 %shard_map.78 = (f32[256,384]{1,0:T(8,128)}, f32[32,1,128]{2,1,0:T(1,128)}) custom-call(f32[256,384]{1,0:T(8,128)} %get-tuple-element.7.gmain, bf16[3,16,384]{2,1,0:T(8,128)(2,1)} %get-tuple-element.8.hrecv, f32[32,1,128]{2,1,0:T(1,128)} %bitcast.10), custom_call_target="tpu_custom_call" | custom-call | tf_op jit(solution)/shard_map/pallas_call | solution.py:411

commit v2 on v1

--- a/solution.py
+++ b/solution.py
@@ -40,7 +40,7 @@
     gmain, hrecv, dep_out,
     edge, innov, rinv, meta,
     tbl, met, jrecv, dep, part, gsend, rbuf, hsend,
-    f_send, f_recv, e_send, e_recv, m_send, m_recv, j_send, j_recv, d_send, d_recv,
+    f_local, f_send, f_recv, e_send, e_recv, m_send, m_recv, j_send, j_recv, d_send, d_recv,
     g_send, g_recv, h_send, h_recv, from_low, from_high,
 ):
     inner = lon_n // line
@@ -66,6 +66,12 @@
     def landed(like, sem):
         pltpu.make_async_copy(like, like, sem).wait()
 
+    def pieces(size):
+        cut = -(-size // 32) * 16
+        return (pl.ds(0, cut), pl.ds(cut, size - cut))
+
+    field_pieces, table_pieces = pieces(cells), pieces(cells + cols + 2 * rows)
+
     def mate(i):
         to = (here + i) % plane
         return to, (to // inner, z * inner + to % inner)
@@ -90,11 +96,21 @@
     lax.fori_loop(1, plane, greet, 0)
 
     own_field = tbl.at[z, pl.ds(0, cells)]
-    pltpu.make_async_copy(field, own_field, f_recv.at[z]).start()
+    local = pltpu.make_async_copy(field, own_field, f_local)
+    local.start()
     for g in visits:
         pltpu.make_async_copy(
             jac.at[lat, g, xi], jrecv.at[g, pl.ds(0, slots)], j_recv.at[g]
         ).start()
+
+    @pl.when(jnp.logical_not(has_low))
+    def _():
+        rbuf[z] = jnp.zeros(rbuf.shape[1:], rbuf.dtype)
+
+    @pl.when(jnp.logical_not(has_high))
+    def _():
+        rbuf[line] = jnp.zeros(rbuf.shape[1:], rbuf.dtype)
+
     innov[...] = innov_ref[...].astype(jnp.float32)
     rinv[...] = rinv_ref[...].astype(jnp.float32)
 
@@ -119,24 +135,25 @@
         return carry
 
     lax.fori_loop(0, plane, build, 0)
-    landed(own_field, f_recv.at[z])
+    local.wait()
     edge[...] = jnp.concatenate(
         [tbl[z, pl.ds(r * cols, cols), :].astype(jnp.float32)[0:1] for r in range(rows)], axis=0
     ).astype(edge.dtype)
     pltpu.make_async_copy(meta.at[0], met.at[:, :, pl.ds(0, slots)], m_recv).start()
     pl.semaphore_wait(barrier, plane - 1 + has_low.astype(jnp.int32) + has_high.astype(jnp.int32))
 
-    def send_field(g, up):
-        piece = tbl.at[g, pl.ds(0, cells)]
-        remote(piece, piece, f_send, f_recv.at[g], high if up else low).start()
-
-    @pl.when(has_low)
-    def _():
-        send_field(z, False)
-
-    @pl.when(has_high)
-    def _():
-        send_field(z, True)
+    def send_field(g, c, up):
+        piece = tbl.at[g, field_pieces[c]]
+        remote(piece, piece, f_send, f_recv.at[g, c], high if up else low).start()
+
+    for c in range(2):
+        @pl.when(has_low)
+        def _():
+            send_field(z, c, False)
+
+        @pl.when(has_high)
+        def _():
+            send_field(z, c, True)
 
     def send_meta(i, carry):
         place = pl.ds(pl.multiple_of(i * slots, slots), slots)
@@ -157,7 +174,7 @@
         return one
 
     lax.fori_loop(1, plane, send_meta, 0)
-    lax.fori_loop(1, plane // 2, send_jac(0), 0)
+    lax.fori_loop(1, plane, send_jac(0), 0)
 
     for _ in range(line - 1):
         @pl.when(has_low)
@@ -184,20 +201,23 @@
                e_recv.at[z_low], (lat, to * inner + x_low)).start()
         remote(edge, tbl.at[z_low, pl.ds(halo + rows, rows)], e_send,
                e_recv.at[z_low], (lat_down, to * inner + x_low)).start()
-    lax.fori_loop(plane // 2, plane, send_jac(0), 0)
     for n in range(1, line):
         lax.fori_loop(1, plane, send_jac(n), 0)
 
+    def field_landed(g, c):
+        landed(tbl.at[g, field_pieces[c]], f_recv.at[g, c])
+
     def forward(d):
-        @pl.when(inside_line & (z >= d))
-        def _():
-            landed(own_field, f_recv.at[z - d])
-            send_field(z - d, True)
-
-        @pl.when(inside_line & (z + d < line))
-        def _():
-            landed(own_field, f_recv.at[z + d])
-            send_field(z + d, False)
+        for c in range(2):
+            @pl.when(inside_line & (z >= d))
+            def _():
+                field_landed(z - d, c)
+                send_field(z - d, c, True)
+
+            @pl.when(inside_line & (z + d < line))
+            def _():
+                field_landed(z + d, c)
+                send_field(z + d, c, False)
 
     landed(met, m_recv)
     inside = jnp.where(lat < lat_n - 1, 1.0, 0.0)
@@ -205,46 +225,45 @@
     tiles = plane // tile
     pad = -(-(max(rows, cols) + 1) // 8) * 8
 
+    def terms(g, t):
+        lanes = pl.ds(pl.multiple_of(t * width, width), width)
+        info = met[g, :, lanes].astype(jnp.float32)
+        lat_w = weight_rows(info[0:1], info[2:3], pad)
+        lon_w = weight_rows(info[1:2], info[3:4], pad)
+        lon_c = lon_w[:cols]
+        lon_e = lon_w[cols:cols + 1]
+        lat_n_row = lat_w[rows:rows + 1] * inside
+        first = lax.broadcasted_iota(jnp.int32, (rows, width), 0) == 0
+        blocks = [lat_w[r:r + 1] * lon_c for r in range(rows)]
+        blocks.append(lat_n_row * lon_c)
+        blocks.append(lat_w[:rows] * lon_e)
+        blocks.append(
+            jnp.where(first, jnp.broadcast_to(lat_n_row * lon_e, (rows, width)), 0.0)
+        )
+        spread = jnp.concatenate(blocks, axis=0).astype(jnp.bfloat16).astype(jnp.float32)
+        jac_t = jrecv[g, lanes]
+        products = lax.dot_general(
+            tbl[g], jac_t, (((1,), (1,)), ((), ())), preferred_element_type=jnp.float32
+        )
+        evolved = jnp.sum(spread * products, axis=0, keepdims=True)
+        departure = jnp.where(info[0:1] >= 0.0, evolved - info[4:5], 0.0)
+        dep[g, :, lanes] = departure
+        return (spread * (info[5:6] * departure)).astype(jnp.bfloat16), jac_t
+
     def compute(n, g):
         into = part.at[n]
+
+        def one_tile(t, carry):
+            scaled, jac_t = terms(g, t)
+            into[...] += jnp.dot(scaled, jac_t, preferred_element_type=jnp.float32)
+            return carry
+
         if tiles > 1:
             into[...] = jnp.zeros(into.shape, into.dtype)
-
-        def one_tile(t, carry):
-            lanes = pl.ds(pl.multiple_of(t * width, width), width)
-            info = met[g, :, lanes].astype(jnp.float32)
-            lat_w = weight_rows(info[0:1], info[2:3], pad)
-            lon_w = weight_rows(info[1:2], info[3:4], pad)
-            lon_c = lon_w[:cols]
-            lon_e = lon_w[cols:cols + 1]
-            lat_n_row = lat_w[rows:rows + 1] * inside
-            first = lax.broadcasted_iota(jnp.int32, (rows, width), 0) == 0
-            blocks = [lat_w[r:r + 1] * lon_c for r in range(rows)]
-            blocks.append(lat_n_row * lon_c)
-            blocks.append(lat_w[:rows] * lon_e)
-            blocks.append(
-                jnp.where(first, jnp.broadcast_to(lat_n_row * lon_e, (rows, width)), 0.0)
-            )
-            spread = jnp.concatenate(blocks, axis=0).astype(jnp.bfloat16).astype(jnp.float32)
-            jac_t = jrecv[g, lanes]
-            products = lax.dot_general(
-                tbl[g], jac_t, (((1,), (1,)), ((), ())), preferred_element_type=jnp.float32
-            )
-            evolved = jnp.sum(spread * products, axis=0, keepdims=True)
-            departure = jnp.where(info[0:1] >= 0.0, evolved - info[4:5], 0.0)
-            dep[g, :, lanes] = departure
-            scaled = (spread * (info[5:6] * departure)).astype(jnp.bfloat16)
-            partial = jnp.dot(scaled, jac_t, preferred_element_type=jnp.float32)
-            if tiles > 1:
-                into[...] += partial
-            else:
-                into[...] = partial
-            return carry
-
-        if tiles > 1:
             lax.fori_loop(0, tiles, one_tile, 0)
         else:
-            one_tile(0, 0)
+            scaled, jac_t = terms(g, 0)
+            into[...] = jnp.dot(scaled, jac_t, preferred_element_type=jnp.float32)
 
     def send_dep(g):
         def one(i, carry):
@@ -261,16 +280,17 @@
 
     def finish(n, incoming):
         g = visits[n]
-        total = part[n]
-        if incoming:
-            landed(rbuf.at[g], g_recv.at[g])
-            total = total + rbuf[g].astype(jnp.float32)
-        gsend[n] = total.astype(gsend.dtype)
         up = g > z
         next_z = jnp.where(up, z + 1, z - 1)
         slot = jnp.where((g == next_z) & jnp.logical_not(up), line, g)
-        remote(gsend.at[n], rbuf.at[slot], g_send, g_recv.at[slot],
-               (lat, next_z * inner + xi)).start()
+        for c, at in enumerate(table_pieces):
+            total = part[n, at, :]
+            if incoming:
+                landed(rbuf.at[g, at], g_recv.at[g, c])
+                total = total + rbuf[g, at, :].astype(jnp.float32)
+            gsend[n, at, :] = total.astype(gsend.dtype)
+            remote(gsend.at[n, at], rbuf.at[slot, at], g_send, g_recv.at[slot, c],
+                   (lat, next_z * inner + xi)).start()
 
     def pass_on(n):
         @pl.when(inside_line)
@@ -279,45 +299,67 @@
 
     for d in range(1, max(line // 2, 1)):
         forward(d)
-    for n in range(line):
+    for n in range(line - 1):
         g = visits[n]
-        if n < line - 1:
-            @pl.when(jnp.logical_not(inside_line))
-            def _():
-                landed(own_field, f_recv.at[g])
+
+        @pl.when(jnp.logical_not(inside_line))
+        def _():
+            for c in range(2):
+                field_landed(g, c)
+
         landed(tbl.at[g, pl.ds(cells, cols + 2 * rows)], e_recv.at[g])
         landed(jrecv.at[g], j_recv.at[g])
         compute(n, g)
         send_dep(g)
-        if n < line - 1:
-            @pl.when(jnp.logical_not(inside_line))
-            def _():
-                finish(n, False)
+
+        @pl.when(jnp.logical_not(inside_line))
+        def _():
+            finish(n, False)
+
         if n == 0:
             for d in range(max(line // 2, 1), line - 1):
                 forward(d)
-        elif n == 1 and n < line - 1:
+        elif n == 1:
             pass_on(0)
             pass_on(1)
-        elif n < line - 1:
+        else:
             pass_on(n)
 
-    @pl.when(has_low)
-    def _():
-        landed(rbuf.at[z], g_recv.at[z])
-        part[line - 1] += rbuf[z].astype(jnp.float32)
-
-    @pl.when(has_high)
-    def _():
-        landed(rbuf.at[line], g_recv.at[line])
-        part[line - 1] += rbuf[line].astype(jnp.float32)
-
-    hsend[...] = part[line - 1, pl.ds(cells, cols + 2 * rows), :].astype(hsend.dtype)
-    remote(hsend.at[pl.ds(0, cols)], hrecv.at[0], h_send, h_recv, (lat_up, lon)).start()
-    remote(hsend.at[pl.ds(cols, rows)], hrecv.at[1], h_send, h_recv, (lat, lon_up)).start()
-    remote(hsend.at[pl.ds(cols + rows, rows)], hrecv.at[2], h_send, h_recv,
-           (lat_up, lon_up)).start()
-    gmain[...] = part[line - 1, pl.ds(0, cells), :]
+    main, rim = pl.ds(0, cells), pl.ds(cells, cols + 2 * rows)
+    landed(tbl.at[z, rim], e_recv.at[z])
+    landed(jrecv.at[z], j_recv.at[z])
+
+    def arrived(at):
+        return rbuf[z, at, :].astype(jnp.float32) + rbuf[line, at, :].astype(jnp.float32)
+
+    def send_rim(values):
+        for c, at in enumerate(table_pieces):
+            @pl.when(has_low)
+            def _():
+                landed(rbuf.at[z, at], g_recv.at[z, c])
+
+            @pl.when(has_high)
+            def _():
+                landed(rbuf.at[line, at], g_recv.at[line, c])
+
+        hsend[...] = (values + arrived(rim)).astype(hsend.dtype)
+        remote(hsend.at[pl.ds(cols + rows, rows)], hrecv.at[2], h_send, h_recv,
+               (lat_up, lon_up)).start()
+        remote(hsend.at[pl.ds(cols, rows)], hrecv.at[1], h_send, h_recv, (lat, lon_up)).start()
+        remote(hsend.at[pl.ds(0, cols)], hrecv.at[0], h_send, h_recv, (lat_up, lon)).start()
+
+    if tiles > 1:
+        compute(line - 1, z)
+        send_rim(part[line - 1, rim, :])
+        send_dep(z)
+        gmain[...] = part[line - 1, main, :] + arrived(main)
+    else:
+        scaled, jac_t = terms(z, 0)
+        send_rim(jnp.dot(scaled[cells:], jac_t, preferred_element_type=jnp.float32))
+        send_dep(z)
+        gmain[...] = arrived(main) + jnp.dot(
+            scaled[:cells], jac_t, preferred_element_type=jnp.float32
+        )
 
     others = pl.ds(0, (plane - 1) * slots)
     for up in (False, True):
@@ -365,13 +407,13 @@
     dma = pltpu.SemaphoreType.DMA
     one = pltpu.SemaphoreType.DMA(())
     vmem = pl.BlockSpec(memory_space=pltpu.VMEM)
-    anywhere = pl.BlockSpec(memory_space=pl.ANY)
+    anywhere = pl.BlockSpec(memory_space=pltpu.HBM)
     parts = pl.pallas_call(
         functools.partial(kernel, lat_n, lon_n, line, rows, cols, tile),
         out_shape=(
-            jax.ShapeDtypeStruct((cells, wide), f32),
-            jax.ShapeDtypeStruct((3, rows, wide), bf16),
-            jax.ShapeDtypeStruct((lat_n, line, inner, 1, slots), f32),
+            pltpu.VMEM((cells, wide), f32),
+            pltpu.VMEM((3, rows, wide), bf16),
+            pltpu.VMEM((lat_n, line, inner, 1, slots), f32),
         ),
         in_specs=[anywhere, vmem, vmem, vmem, vmem, anywhere],
         out_specs=(vmem,) * 3,
@@ -388,17 +430,17 @@
             pltpu.VMEM((line - 1, table, wide), bf16),
             pltpu.VMEM((line + 1, table, wide), bf16),
             pltpu.VMEM((table - cells, wide), bf16),
-            one, dma((line,)),
+            one, one, dma((line, 2)),
             one, dma((line,)),
             one, one,
             one, dma((line,)),
             one, one,
-            one, dma((line + 1,)),
+            one, dma((line + 1, 2)),
             one, one,
             pltpu.SemaphoreType.REGULAR, pltpu.SemaphoreType.REGULAR,
         ],
         compiler_params=pltpu.CompilerParams(
-            collective_id=0, has_side_effects=True, vmem_limit_bytes=60 * 1024 * 1024
+            collective_id=0, has_side_effects=True, vmem_limit_bytes=62 * 1024 * 1024
         ),
     )(
         field.reshape(cells, wide),
@@ -416,6 +458,7 @@
         ),
         in_specs=[vmem] * 3,
         out_specs=(vmem, vmem),
+        compiler_params=pltpu.CompilerParams(vmem_limit_bytes=8 * 1024 * 1024),
     )(*parts[:2], parts[2].reshape(total, 1, slots))
     return departures, grad.reshape(rows, cols, wide)
 

time: 55.4 us -> 52 us (0.939)
  the two profiles are of different devices: /device:TPU:9 before, /device:TPU:0 now
where the time goes in v2:
time: 52 us; the launch traced here: 51.7 us
  Pallas kernels  51.1 us (98%)
  between operations  0.64 us (1%)
    pallas_call x1, Pallas kernels, shards(): pl.pallas_call(functools.partial(kernel, lat_n, lon_n, line, rows, cols,...  50.3 us

profile of v2, /device:TPU:0, one launch (start us, length us, event | category | flops | bytes accessed | tf_op | source)
XLA Modules:
  0.0 51.7 jit_solution(15218068306973459907)
XLA Ops:
  0.6 50.3 %shard_map.77 = (f32[256,384]{1,0:T(8,128)S(1)}, bf16[3,16,384]{2,1,0:T(8,128)(2,1)S(1)}, f32[4,4,2,1,128]{4,3,2,1,0:T(1,128)S(1)}) custom-call(bf16[256,384]{1,0:T(8,128)(2,1)} %bitcast.9, s32[32,1,128]{2,1,0:T(1,128)} %cell_ref.1, bf16[32,2,128]{2,1,0:T(2,128)(2,1)} %bitcast.10, bf16[32,128]{1,0:T(8,128)(2,1)} %bitcast.11, bf16[32,128]{1,0:T(8,128)(2,1)} %bitcast.12, ...), custom_call_target="tpu_custom_call" | custom-call | tf_op jit(solution)/shard_map/pallas_call | solution.py:411
  50.9 0.8 %shard_map.78 = (f32[256,384]{1,0:T(8,128)}, f32[32,1,128]{2,1,0:T(1,128)}) custom-call(f32[256,384]{1,0:T(8,128)S(1)} %get-tuple-element.7.gmain, bf16[3,16,384]{2,1,0:T(8,128)(2,1)S(1)} %get-tuple-element.8.hrecv, f32[32,1,128]{2,1,0:T(1,128)S(1)} %bitcast.7), custom_call_target="tpu_custom_call" | custom-call | tf_op jit(solution)/shard_map/pallas_call | solution.py:453

commit v3 on v2

--- a/solution.py
+++ b/solution.py
@@ -40,7 +40,7 @@
     gmain, hrecv, dep_out,
     edge, innov, rinv, meta,
     tbl, met, jrecv, dep, part, gsend, rbuf, hsend,
-    f_local, f_send, f_recv, e_send, e_recv, m_send, m_recv, j_send, j_recv, d_send, d_recv,
+    f_local, f_send, f_recv, e_send, e_own, b_send, e_recv, m_send, m_recv, j_send, j_recv, d_send, d_recv,
     g_send, g_recv, h_send, h_recv, from_low, from_high,
 ):
     inner = lon_n // line
@@ -100,7 +100,7 @@
     local.start()
     for g in visits:
         pltpu.make_async_copy(
-            jac.at[lat, g, xi], jrecv.at[g, pl.ds(0, slots)], j_recv.at[g]
+            jac.at[lat, g, xi], jrecv.at[g, pl.ds(0, slots)], j_recv.at[g, 0]
         ).start()
 
     @pl.when(jnp.logical_not(has_low))
@@ -110,6 +110,20 @@
     @pl.when(jnp.logical_not(has_high))
     def _():
         rbuf[line] = jnp.zeros(rbuf.shape[1:], rbuf.dtype)
+
+    has_south, has_north = lat > 0, lat < lat_n - 1
+    row_rim, edge_rim = pl.ds(cells, cols), pl.ds(halo, rows)
+    corner_rim, rim = pl.ds(halo + rows, rows), pl.ds(cells, cols + 2 * rows)
+
+    @pl.when(jnp.logical_not(has_north))
+    def _():
+        tbl[z, row_rim, :] = jnp.zeros((cols, tbl.shape[2]), tbl.dtype)
+        tbl[z, corner_rim, :] = jnp.zeros((rows, tbl.shape[2]), tbl.dtype)
+
+    @pl.when(jnp.logical_not(has_south))
+    def _():
+        hrecv[0] = jnp.zeros(hrecv.shape[1:], hrecv.dtype)
+        hrecv[2] = jnp.zeros(hrecv.shape[1:], hrecv.dtype)
 
     innov[...] = innov_ref[...].astype(jnp.float32)
     rinv[...] = rinv_ref[...].astype(jnp.float32)
@@ -146,20 +160,16 @@
         piece = tbl.at[g, field_pieces[c]]
         remote(piece, piece, f_send, f_recv.at[g, c], high if up else low).start()
 
-    for c in range(2):
-        @pl.when(has_low)
-        def _():
-            send_field(z, c, False)
-
-        @pl.when(has_high)
-        def _():
-            send_field(z, c, True)
-
     def send_meta(i, carry):
         place = pl.ds(pl.multiple_of(i * slots, slots), slots)
         remote(meta.at[i], met.at[:, :, place], m_send, m_recv, mate(i)[1]).start()
         return carry
 
+    half = plane // 2
+
+    def jac_landed(g, h):
+        landed(jrecv.at[g, pl.ds(h * half * slots, half * slots)], j_recv.at[g, h])
+
     def send_jac(n):
         g = visits[n]
 
@@ -167,14 +177,42 @@
             to, at = mate(i)
             place = pl.ds(pl.multiple_of(i * slots, slots), slots)
             remote(
-                jac.at[to // inner, g, to % inner], jrecv.at[g, place], j_send, j_recv.at[g], at
+                jac.at[to // inner, g, to % inner], jrecv.at[g, place], j_send,
+                j_recv.at[g, i // half], at
             ).start()
             return carry
 
         return one
 
+    def send_edge():
+        remote(edge, tbl.at[z_low, edge_rim], e_send, e_own, (lat, lon_down)).start()
+
+        @pl.when(has_south)
+        def _():
+            remote(edge, tbl.at[z_low, corner_rim], e_send, e_own, (lat_down, lon_down)).start()
+
+    early = plane - plane // 4
     lax.fori_loop(1, plane, send_meta, 0)
-    lax.fori_loop(1, plane, send_jac(0), 0)
+    lax.fori_loop(1, 3, send_jac(0), 0)
+    for c in range(2):
+        @pl.when(has_low)
+        def _():
+            send_field(z, c, False)
+
+        @pl.when(has_high)
+        def _():
+            send_field(z, c, True)
+
+    @pl.when(has_south)
+    def _():
+        remote(tbl.at[z, pl.ds(0, cols)], tbl.at[z, row_rim], e_send, e_own,
+               (lat_down, lon)).start()
+
+    @pl.when(xi > 0)
+    def _():
+        send_edge()
+
+    lax.fori_loop(3, early, send_jac(0), 0)
 
     for _ in range(line - 1):
         @pl.when(has_low)
@@ -193,14 +231,11 @@
         def _():
             pl.semaphore_wait(from_high, 1)
 
-    for i in range(line):
-        to = (z + i) % line
-        remote(tbl.at[z, pl.ds(0, cols)], tbl.at[z, pl.ds(cells, cols)], e_send,
-               e_recv.at[z], (lat_down, to * inner + xi)).start()
-        remote(edge, tbl.at[z_low, pl.ds(halo, rows)], e_send,
-               e_recv.at[z_low], (lat, to * inner + x_low)).start()
-        remote(edge, tbl.at[z_low, pl.ds(halo + rows, rows)], e_send,
-               e_recv.at[z_low], (lat_down, to * inner + x_low)).start()
+    @pl.when(xi == 0)
+    def _():
+        send_edge()
+
+    lax.fori_loop(early, plane, send_jac(0), 0)
     for n in range(1, line):
         lax.fori_loop(1, plane, send_jac(n), 0)
 
@@ -219,13 +254,12 @@
                 field_landed(z + d, c)
                 send_field(z + d, c, False)
 
-    landed(met, m_recv)
     inside = jnp.where(lat < lat_n - 1, 1.0, 0.0)
     width = tile * slots
     tiles = plane // tile
     pad = -(-(max(rows, cols) + 1) // 8) * 8
 
-    def terms(g, t):
+    def terms(g, t, width):
         lanes = pl.ds(pl.multiple_of(t * width, width), width)
         info = met[g, :, lanes].astype(jnp.float32)
         lat_w = weight_rows(info[0:1], info[2:3], pad)
@@ -254,7 +288,7 @@
         into = part.at[n]
 
         def one_tile(t, carry):
-            scaled, jac_t = terms(g, t)
+            scaled, jac_t = terms(g, t, width)
             into[...] += jnp.dot(scaled, jac_t, preferred_element_type=jnp.float32)
             return carry
 
@@ -262,10 +296,10 @@
             into[...] = jnp.zeros(into.shape, into.dtype)
             lax.fori_loop(0, tiles, one_tile, 0)
         else:
-            scaled, jac_t = terms(g, 0)
+            scaled, jac_t = terms(g, 0, width)
             into[...] = jnp.dot(scaled, jac_t, preferred_element_type=jnp.float32)
 
-    def send_dep(g):
+    def send_dep(g, first, last):
         def one(i, carry):
             to = (here + plane - i) % plane
             place = pl.ds(pl.multiple_of(i * slots, slots), slots)
@@ -275,8 +309,11 @@
             ).start()
             return carry
 
-        lax.fori_loop(1, plane, one, 0)
-        pltpu.make_async_copy(dep.at[g, :, pl.ds(0, slots)], dep_out.at[lat, g, xi], d_recv).start()
+        lax.fori_loop(max(first, 1), last, one, 0)
+        if first == 0:
+            pltpu.make_async_copy(
+                dep.at[g, :, pl.ds(0, slots)], dep_out.at[lat, g, xi], d_recv
+            ).start()
 
     def finish(n, incoming):
         g = visits[n]
@@ -299,6 +336,19 @@
 
     for d in range(1, max(line // 2, 1)):
         forward(d)
+
+    @pl.when(has_north)
+    def _():
+        landed(tbl.at[z, rim], e_own)
+
+    @pl.when(jnp.logical_not(has_north))
+    def _():
+        landed(edge, e_own)
+
+    for i in range(1, line):
+        remote(tbl.at[z, rim], tbl.at[z, rim], b_send, e_recv.at[z],
+               (lat, (z + i) % line * inner + xi)).start()
+    landed(met, m_recv)
     for n in range(line - 1):
         g = visits[n]
 
@@ -307,10 +357,11 @@
             for c in range(2):
                 field_landed(g, c)
 
-        landed(tbl.at[g, pl.ds(cells, cols + 2 * rows)], e_recv.at[g])
-        landed(jrecv.at[g], j_recv.at[g])
+        landed(tbl.at[g, rim], e_recv.at[g])
+        jac_landed(g, 0)
+        jac_landed(g, 1)
         compute(n, g)
-        send_dep(g)
+        send_dep(g, 0, plane)
 
         @pl.when(jnp.logical_not(inside_line))
         def _():
@@ -325,9 +376,7 @@
         else:
             pass_on(n)
 
-    main, rim = pl.ds(0, cells), pl.ds(cells, cols + 2 * rows)
-    landed(tbl.at[z, rim], e_recv.at[z])
-    landed(jrecv.at[z], j_recv.at[z])
+    main = pl.ds(0, cells)
 
     def arrived(at):
         return rbuf[z, at, :].astype(jnp.float32) + rbuf[line, at, :].astype(jnp.float32)
@@ -343,21 +392,33 @@
                 landed(rbuf.at[line, at], g_recv.at[line, c])
 
         hsend[...] = (values + arrived(rim)).astype(hsend.dtype)
-        remote(hsend.at[pl.ds(cols + rows, rows)], hrecv.at[2], h_send, h_recv,
-               (lat_up, lon_up)).start()
         remote(hsend.at[pl.ds(cols, rows)], hrecv.at[1], h_send, h_recv, (lat, lon_up)).start()
-        remote(hsend.at[pl.ds(0, cols)], hrecv.at[0], h_send, h_recv, (lat_up, lon)).start()
+
+        @pl.when(has_north)
+        def _():
+            remote(hsend.at[pl.ds(cols + rows, rows)], hrecv.at[2], h_send, h_recv,
+                   (lat_up, lon_up)).start()
+            remote(hsend.at[pl.ds(0, cols)], hrecv.at[0], h_send, h_recv, (lat_up, lon)).start()
 
     if tiles > 1:
+        jac_landed(z, 0)
+        jac_landed(z, 1)
         compute(line - 1, z)
         send_rim(part[line - 1, rim, :])
-        send_dep(z)
+        send_dep(z, 0, plane)
         gmain[...] = part[line - 1, main, :] + arrived(main)
     else:
-        scaled, jac_t = terms(z, 0)
-        send_rim(jnp.dot(scaled[cells:], jac_t, preferred_element_type=jnp.float32))
-        send_dep(z)
-        gmain[...] = arrived(main) + jnp.dot(
+        jac_landed(z, 0)
+        scaled, jac_t = terms(z, 0, half * slots)
+        part[line - 1] = jnp.dot(scaled, jac_t, preferred_element_type=jnp.float32)
+        send_dep(z, 0, half)
+        jac_landed(z, 1)
+        scaled, jac_t = terms(z, 1, half * slots)
+        send_rim(part[line - 1, rim, :] + jnp.dot(
+            scaled[cells:], jac_t, preferred_element_type=jnp.float32
+        ))
+        send_dep(z, half, plane)
+        gmain[...] = arrived(main) + part[line - 1, main, :] + jnp.dot(
             scaled[:cells], jac_t, preferred_element_type=jnp.float32
         )
 
@@ -369,13 +430,35 @@
             @pl.when(sent & (inside_line | (i == 0)))
             def _():
                 landed(own_field, f_send)
-    landed(tbl.at[:, pl.ds(cells, cols + 2 * rows)], e_send)
+    @pl.when(has_south)
+    def _():
+        landed(tbl.at[z, rim], e_send)
+
+    @pl.when(jnp.logical_not(has_south))
+    def _():
+        landed(edge, e_send)
+
+    landed(tbl.at[pl.ds(0, line - 1), rim], b_send)
     landed(met.at[:, :, others], m_send)
     landed(jrecv.at[:, others], j_send)
     landed(dep.at[:, :, others], d_send)
     landed(gsend, g_send)
-    landed(hsend, h_send)
-    landed(hrecv, h_recv)
+    @pl.when(has_north)
+    def _():
+        landed(hsend, h_send)
+
+    @pl.when(jnp.logical_not(has_north))
+    def _():
+        landed(edge, h_send)
+
+    @pl.when(has_south)
+    def _():
+        landed(hrecv, h_recv)
+
+    @pl.when(jnp.logical_not(has_south))
+    def _():
+        landed(edge, h_recv)
+
     landed(dep_out, d_recv)
 
 
@@ -431,9 +514,9 @@
             pltpu.VMEM((line + 1, table, wide), bf16),
             pltpu.VMEM((table - cells, wide), bf16),
             one, one, dma((line, 2)),
-            one, dma((line,)),
+            one, one, one, dma((line,)),
             one, one,
-            one, dma((line,)),
+            one, dma((line, 2)),
             one, one,
             one, dma((line + 1, 2)),
             one, one,

time: 52 us -> 49.6 us (0.954)
  Pallas kernels: 51.1 us -> 48.7 us
    pallas_call x1, Pallas kernels: 50.3 us -> 47.9 us  [shards(): pl.pallas_call(functools.partial(kernel, lat_n, lon_n, line, rows, cols,...]
where the time goes in v3:
time: 49.6 us; the launch traced here: 49.3 us
  Pallas kernels  48.7 us (98%)
  between operations  0.64 us (1%)
    pallas_call x1, Pallas kernels, shards(): pl.pallas_call(functools.partial(kernel, lat_n, lon_n, line, rows, cols,...  47.9 us

profile of v3, /device:TPU:0, one launch (start us, length us, event | category | flops | bytes accessed | tf_op | source)
XLA Modules:
  0.0 49.3 jit_solution(2876829853032045080)
XLA Ops:
  0.6 47.9 %shard_map.77 = (f32[256,384]{1,0:T(8,128)S(1)}, bf16[3,16,384]{2,1,0:T(8,128)(2,1)S(1)}, f32[4,4,2,1,128]{4,3,2,1,0:T(1,128)S(1)}) custom-call(bf16[256,384]{1,0:T(8,128)(2,1)} %bitcast.9, s32[32,1,128]{2,1,0:T(1,128)} %cell_ref.1, bf16[32,2,128]{2,1,0:T(2,128)(2,1)} %bitcast.10, bf16[32,128]{1,0:T(8,128)(2,1)} %bitcast.11, bf16[32,128]{1,0:T(8,128)(2,1)} %bitcast.12, ...), custom_call_target="tpu_custom_call" | custom-call | tf_op jit(solution)/shard_map/pallas_call | solution.py:494
  48.5 0.8 %shard_map.78 = (f32[256,384]{1,0:T(8,128)}, f32[32,1,128]{2,1,0:T(1,128)}) custom-call(f32[256,384]{1,0:T(8,128)S(1)} %get-tuple-element.7.gmain, bf16[3,16,384]{2,1,0:T(8,128)(2,1)S(1)} %get-tuple-element.8.hrecv, f32[32,1,128]{2,1,0:T(1,128)S(1)} %bitcast.7), custom_call_target="tpu_custom_call" | custom-call | tf_op jit(solution)/shard_map/pallas_call | solution.py:536

commit v4 on v3

--- a/solution.py
+++ b/solution.py
@@ -38,9 +38,9 @@
     lat_n, lon_n, line, rows, cols, tile,
     field, cell_ref, frac_ref, innov_ref, rinv_ref, jac,
     gmain, hrecv, dep_out,
-    edge, innov, rinv, meta,
+    edge, innov, rinv, meta, lent,
     tbl, met, jrecv, dep, part, gsend, rbuf, hsend,
-    f_local, f_send, f_recv, e_send, e_own, b_send, e_recv, m_send, m_recv, j_send, j_recv, d_send, d_recv,
+    f_local, f_send, f_recv, e_send, e_own, b_send, e_recv, m_send, m_recv, l_send, l_recv, s_send, s_recv, j_send, j_recv, d_send, d_recv,
     g_send, g_recv, h_send, h_recv, from_low, from_high,
 ):
     inner = lon_n // line
@@ -66,15 +66,27 @@
     def landed(like, sem):
         pltpu.make_async_copy(like, like, sem).wait()
 
-    def pieces(size):
-        cut = -(-size // 32) * 16
-        return (pl.ds(0, cut), pl.ds(cut, size - cut))
-
-    field_pieces, table_pieces = pieces(cells), pieces(cells + cols + 2 * rows)
+    def pieces(size, count):
+        cuts = [-(-size * c // (16 * count)) * 16 for c in range(count)] + [size]
+        return [pl.ds(a, b - a) for a, b in zip(cuts, cuts[1:])]
+
+    field_pieces = pieces(cells, f_recv.shape[1])
+    table_pieces = [pl.ds(cells, cols + 2 * rows), *pieces(cells, g_recv.shape[1] - 1)]
 
     def mate(i):
-        to = (here + i) % plane
-        return to, (to // inner, z * inner + to % inner)
+        to_lat, to_x = (lat + i // inner) % lat_n, (xi + i % inner) % inner
+        return to_lat, to_x, (to_lat, z * inner + to_x)
+
+    def lent_out(i, g):
+        return (z == line - 1) & (i == moved) & (g == there)
+
+    def source(i):
+        return (lat + lat_n - i // inner) % lat_n, (xi + inner - i % inner) % inner
+
+    moved = (lat_n // 2) * inner + inner // 2
+    there = jnp.where(lat % 2 == 0, line - 2, max(line - 3, 0))
+    lender, taker = z == line - 1, z == there
+    spare = pl.ds(plane * slots, slots)
 
     has_low, has_high = z > 0, z < line - 1
     inside_line = has_low & has_high
@@ -90,7 +102,7 @@
         pl.semaphore_signal(barrier, inc=1, device_id=high, device_id_type=MESH)
 
     def greet(i, carry):
-        pl.semaphore_signal(barrier, inc=1, device_id=mate(i)[1], device_id_type=MESH)
+        pl.semaphore_signal(barrier, inc=1, device_id=mate(i)[2], device_id_type=MESH)
         return carry
 
     lax.fori_loop(1, plane, greet, 0)
@@ -129,9 +141,9 @@
     rinv[...] = rinv_ref[...].astype(jnp.float32)
 
     def build(i, carry):
-        to, _ = mate(i)
+        to_lat, to_x, _ = mate(i)
         for g in range(line):
-            owner = (to // inner) * lon_n + g * inner + to % inner
+            owner = to_lat * lon_n + g * inner + to_x
             cell = cell_ref[owner].astype(jnp.float32)
             live = cell >= 0.0
             row = jnp.floor((cell + 0.5) * (1.0 / (cols + 1)))
@@ -149,6 +161,15 @@
         return carry
 
     lax.fori_loop(0, plane, build, 0)
+
+    @pl.when(lender)
+    def _():
+        lent[...] = meta[moved, there]
+        meta[moved, there] = jnp.full(lent.shape, AWAY, lent.dtype)
+        jrecv[there, pl.ds(moved * slots, slots), :] = jnp.zeros(
+            (slots, jrecv.shape[2]), jrecv.dtype
+        )
+
     local.wait()
     edge[...] = jnp.concatenate(
         [tbl[z, pl.ds(r * cols, cols), :].astype(jnp.float32)[0:1] for r in range(rows)], axis=0
@@ -162,7 +183,7 @@
 
     def send_meta(i, carry):
         place = pl.ds(pl.multiple_of(i * slots, slots), slots)
-        remote(meta.at[i], met.at[:, :, place], m_send, m_recv, mate(i)[1]).start()
+        remote(meta.at[i], met.at[:, :, place], m_send, m_recv, mate(i)[2]).start()
         return carry
 
     half = plane // 2
@@ -174,12 +195,15 @@
         g = visits[n]
 
         def one(i, carry):
-            to, at = mate(i)
-            place = pl.ds(pl.multiple_of(i * slots, slots), slots)
-            remote(
-                jac.at[to // inner, g, to % inner], jrecv.at[g, place], j_send,
-                j_recv.at[g, i // half], at
-            ).start()
+            @pl.when(jnp.logical_not(lent_out(i, g)))
+            def _():
+                to_lat, to_x, at = mate(i)
+                place = pl.ds(pl.multiple_of(i * slots, slots), slots)
+                remote(
+                    jac.at[to_lat, g, to_x], jrecv.at[g, place], j_send,
+                    j_recv.at[g, i // half], at,
+                ).start()
+
             return carry
 
         return one
@@ -194,12 +218,12 @@
     early = plane - plane // 4
     lax.fori_loop(1, plane, send_meta, 0)
     lax.fori_loop(1, 3, send_jac(0), 0)
-    for c in range(2):
-        @pl.when(has_low)
+    for c in range(len(field_pieces)):
+        @pl.when(has_low & (z >= line // 2))
         def _():
             send_field(z, c, False)
 
-        @pl.when(has_high)
+        @pl.when(has_high & (z < line // 2))
         def _():
             send_field(z, c, True)
 
@@ -239,11 +263,18 @@
     for n in range(1, line):
         lax.fori_loop(1, plane, send_jac(n), 0)
 
+    @pl.when(lender)
+    def _():
+        to_lat, to_x, _ = mate(moved)
+        at = (to_lat, there * inner + to_x)
+        remote(lent, met.at[there, :, spare], l_send, l_recv, at).start()
+        remote(jac.at[to_lat, there, to_x], jrecv.at[there, spare], j_send, s_recv, at).start()
+
     def field_landed(g, c):
         landed(tbl.at[g, field_pieces[c]], f_recv.at[g, c])
 
     def forward(d):
-        for c in range(2):
+        for c in range(len(field_pieces)):
             @pl.when(inside_line & (z >= d))
             def _():
                 field_landed(z - d, c)
@@ -301,12 +332,15 @@
 
     def send_dep(g, first, last):
         def one(i, carry):
-            to = (here + plane - i) % plane
-            place = pl.ds(pl.multiple_of(i * slots, slots), slots)
-            remote(
-                dep.at[g, :, place], dep_out.at[lat, g, xi], d_send, d_recv,
-                (to // inner, z * inner + to % inner),
-            ).start()
+            @pl.when(jnp.logical_not(lent_out(i, g)))
+            def _():
+                to_lat, to_x = source(i)
+                place = pl.ds(pl.multiple_of(i * slots, slots), slots)
+                remote(
+                    dep.at[g, :, place], dep_out.at[lat, g, xi], d_send, d_recv,
+                    (to_lat, z * inner + to_x),
+                ).start()
+
             return carry
 
         lax.fori_loop(max(first, 1), last, one, 0)
@@ -348,18 +382,26 @@
     for i in range(1, line):
         remote(tbl.at[z, rim], tbl.at[z, rim], b_send, e_recv.at[z],
                (lat, (z + i) % line * inner + xi)).start()
-    landed(met, m_recv)
+    landed(met.at[:, :, pl.ds(0, plane * slots)], m_recv)
     for n in range(line - 1):
         g = visits[n]
 
         @pl.when(jnp.logical_not(inside_line))
         def _():
-            for c in range(2):
+            for c in range(len(field_pieces)):
                 field_landed(g, c)
 
         landed(tbl.at[g, rim], e_recv.at[g])
-        jac_landed(g, 0)
-        jac_landed(g, 1)
+        jac_landed(g, 1 - moved // half)
+
+        @pl.when(lent_out(moved, g))
+        def _():
+            landed(jrecv.at[g, pl.ds(slots, (half - 1) * slots)], j_recv.at[g, moved // half])
+
+        @pl.when(jnp.logical_not(lent_out(moved, g)))
+        def _():
+            jac_landed(g, moved // half)
+
         compute(n, g)
         send_dep(g, 0, plane)
 
@@ -370,6 +412,14 @@
         if n == 0:
             for d in range(max(line // 2, 1), line - 1):
                 forward(d)
+            for c in range(len(field_pieces)):
+                @pl.when(has_low & (z < line // 2))
+                def _():
+                    send_field(z, c, False)
+
+                @pl.when(has_high & (z >= line // 2))
+                def _():
+                    send_field(z, c, True)
         elif n == 1:
             pass_on(0)
             pass_on(1)
@@ -381,8 +431,10 @@
     def arrived(at):
         return rbuf[z, at, :].astype(jnp.float32) + rbuf[line, at, :].astype(jnp.float32)
 
-    def send_rim(values):
-        for c, at in enumerate(table_pieces):
+    def sums_landed(first, last):
+        for c in range(first, last):
+            at = table_pieces[c]
+
             @pl.when(has_low)
             def _():
                 landed(rbuf.at[z, at], g_recv.at[z, c])
@@ -391,6 +443,8 @@
             def _():
                 landed(rbuf.at[line, at], g_recv.at[line, c])
 
+    def send_rim(values):
+        sums_landed(0, 1)
         hsend[...] = (values + arrived(rim)).astype(hsend.dtype)
         remote(hsend.at[pl.ds(cols, rows)], hrecv.at[1], h_send, h_recv, (lat, lon_up)).start()
 
@@ -400,27 +454,60 @@
                    (lat_up, lon_up)).start()
             remote(hsend.at[pl.ds(0, cols)], hrecv.at[0], h_send, h_recv, (lat_up, lon)).start()
 
+    def take_spare():
+        landed(met.at[z, :, spare], l_recv)
+        landed(jrecv.at[z, spare], s_recv)
+        return terms(z, plane, slots)
+
+    def return_spare():
+        to_lat, to_x = source(moved)
+        remote(dep.at[z, :, spare], dep_out.at[lat, z, xi], s_send, d_recv,
+               (to_lat, (line - 1) * inner + to_x)).start()
+
+    def add(terms_of):
+        scaled, jac_t = terms_of
+        part[line - 1] += jnp.dot(scaled, jac_t, preferred_element_type=jnp.float32)
+
+    def conclude(terms_of, send_rest):
+        scaled, jac_t = terms_of
+        send_rim(part[line - 1, rim, :] + jnp.dot(
+            scaled[cells:], jac_t, preferred_element_type=jnp.float32
+        ))
+        send_rest()
+        sums_landed(1, len(table_pieces))
+        gmain[...] = arrived(main) + part[line - 1, main, :] + jnp.dot(
+            scaled[:cells], jac_t, preferred_element_type=jnp.float32
+        )
+
+    jac_landed(z, 0)
     if tiles > 1:
-        jac_landed(z, 0)
         jac_landed(z, 1)
         compute(line - 1, z)
+        send_dep(z, 0, plane)
+
+        @pl.when(taker)
+        def _():
+            add(take_spare())
+            return_spare()
+
         send_rim(part[line - 1, rim, :])
-        send_dep(z, 0, plane)
+        sums_landed(1, len(table_pieces))
         gmain[...] = part[line - 1, main, :] + arrived(main)
     else:
-        jac_landed(z, 0)
         scaled, jac_t = terms(z, 0, half * slots)
         part[line - 1] = jnp.dot(scaled, jac_t, preferred_element_type=jnp.float32)
         send_dep(z, 0, half)
         jac_landed(z, 1)
-        scaled, jac_t = terms(z, 1, half * slots)
-        send_rim(part[line - 1, rim, :] + jnp.dot(
-            scaled[cells:], jac_t, preferred_element_type=jnp.float32
-        ))
-        send_dep(z, half, plane)
-        gmain[...] = arrived(main) + part[line - 1, main, :] + jnp.dot(
-            scaled[:cells], jac_t, preferred_element_type=jnp.float32
-        )
+
+        @pl.when(taker)
+        def _():
+            add(terms(z, 1, half * slots))
+            send_dep(z, half, plane)
+            conclude(take_spare(), return_spare)
+
+        @pl.when(jnp.logical_not(taker))
+        def _():
+            conclude(terms(z, 1, half * slots), lambda: send_dep(z, half, plane))
 
     others = pl.ds(0, (plane - 1) * slots)
     for up in (False, True):
@@ -441,7 +528,21 @@
     landed(tbl.at[pl.ds(0, line - 1), rim], b_send)
     landed(met.at[:, :, others], m_send)
     landed(jrecv.at[:, others], j_send)
-    landed(dep.at[:, :, others], d_send)
+    landed(dep.at[pl.ds(0, line - 1), :, others], d_send)
+    landed(dep.at[0, :, pl.ds(0, (plane - 2) * slots)], d_send)
+
+    @pl.when(jnp.logical_not(lender))
+    def _():
+        landed(dep.at[0, :, pl.ds(0, slots)], d_send)
+
+    @pl.when(lender)
+    def _():
+        landed(lent, l_send)
+
+    @pl.when(taker)
+    def _():
+        landed(dep.at[0, :, spare], s_send)
+
     landed(gsend, g_send)
     @pl.when(has_north)
     def _():
@@ -505,10 +606,11 @@
             pltpu.VMEM((total, slots), f32),
             pltpu.VMEM((total, slots), f32),
             pltpu.VMEM((plane, line, 8, slots), bf16),
+            pltpu.VMEM((8, slots), bf16),
             pltpu.VMEM((line, table, wide), bf16),
-            pltpu.VMEM((line, 8, plane * slots), bf16),
-            pltpu.VMEM((line, plane * slots, wide), bf16),
-            pltpu.VMEM((line, 1, plane * slots), f32),
+            pltpu.VMEM((line, 8, (plane + 1) * slots), bf16),
+            pltpu.VMEM((line, (plane + 1) * slots, wide), bf16),
+            pltpu.VMEM((line, 1, (plane + 1) * slots), f32),
             pltpu.VMEM((line, table, wide), f32),
             pltpu.VMEM((line - 1, table, wide), bf16),
             pltpu.VMEM((line + 1, table, wide), bf16),
@@ -516,9 +618,10 @@
             one, one, dma((line, 2)),
             one, one, one, dma((line,)),
             one, one,
+            one, one, one, one,
             one, dma((line, 2)),
             one, one,
-            one, dma((line + 1, 2)),
+            one, dma((line + 1, 3)),
             one, one,
             pltpu.SemaphoreType.REGULAR, pltpu.SemaphoreType.REGULAR,
         ],

time: 49.6 us -> 47.5 us (0.958)
  Pallas kernels: 48.7 us -> 46.6 us
    pallas_call x1, Pallas kernels: 47.9 us -> 45.8 us  [shards(): pl.pallas_call(functools.partial(kernel, lat_n, lon_n, line, rows, cols,...]
where the time goes in v4:
time: 47.5 us; the launch traced here: 47.3 us
  Pallas kernels  46.6 us (98%)
  between operations  0.64 us (1%)
    pallas_call x1, Pallas kernels, shards(): pl.pallas_call(functools.partial(kernel, lat_n, lon_n, line, rows, cols,...  45.8 us

profile of v4, /device:TPU:0, one launch (start us, length us, event | category | flops | bytes accessed | tf_op | source)
XLA Modules:
  0.0 47.3 jit_solution(12048984961221079511)
XLA Ops:
  0.6 45.8 %shard_map.77 = (f32[256,384]{1,0:T(8,128)S(1)}, bf16[3,16,384]{2,1,0:T(8,128)(2,1)S(1)}, f32[4,4,2,1,128]{4,3,2,1,0:T(1,128)S(1)}) custom-call(bf16[256,384]{1,0:T(8,128)(2,1)} %bitcast.9, s32[32,1,128]{2,1,0:T(1,128)} %cell_ref.1, bf16[32,2,128]{2,1,0:T(2,128)(2,1)} %bitcast.10, bf16[32,128]{1,0:T(8,128)(2,1)} %bitcast.11, bf16[32,128]{1,0:T(8,128)(2,1)} %bitcast.12, ...), custom_call_target="tpu_custom_call" | custom-call | tf_op jit(solution)/shard_map/pallas_call | solution.py:595
  46.5 0.8 %shard_map.78 = (f32[256,384]{1,0:T(8,128)}, f32[32,1,128]{2,1,0:T(1,128)}) custom-call(f32[256,384]{1,0:T(8,128)S(1)} %get-tuple-element.7.gmain, bf16[3,16,384]{2,1,0:T(8,128)(2,1)S(1)} %get-tuple-element.8.hrecv, f32[32,1,128]{2,1,0:T(1,128)S(1)} %bitcast.7), custom_call_target="tpu_custom_call" | custom-call | tf_op jit(solution)/shard_map/pallas_call | solution.py:639

commit v5 on v4

--- a/solution.py
+++ b/solution.py
@@ -36,11 +36,12 @@
 
 def kernel(
     lat_n, lon_n, line, rows, cols, tile,
-    field, cell_ref, frac_ref, innov_ref, rinv_ref, jac,
+    field, cell_in, frac_in, innov_in, rinv_in, jac,
     gmain, hrecv, dep_out,
-    edge, innov, rinv, meta, lent,
+    cell_ref, frac_ref, innov_ref, rinv_ref,
+    edge, innov, rinv, rowcol, meta, lent,
     tbl, met, jrecv, dep, part, gsend, rbuf, hsend,
-    f_local, f_send, f_recv, e_send, e_own, b_send, e_recv, m_send, m_recv, l_send, l_recv, s_send, s_recv, j_send, j_recv, d_send, d_recv,
+    f_local, s_local, f_send, f_recv, e_send, e_own, b_send, e_recv, m_send, m_recv, l_send, l_recv, s_send, s_recv, j_send, j_recv, d_send, d_recv,
     g_send, g_recv, h_send, h_recv, from_low, from_high,
 ):
     inner = lon_n // line
@@ -109,7 +110,14 @@
 
     own_field = tbl.at[z, pl.ds(0, cells)]
     local = pltpu.make_async_copy(field, own_field, f_local)
-    local.start()
+    smalls = [
+        pltpu.make_async_copy(src, dst, s_local.at[k])
+        for k, (src, dst) in enumerate((
+            (cell_in, cell_ref), (frac_in, frac_ref), (innov_in, innov_ref), (rinv_in, rinv_ref),
+        ))
+    ]
+    for copy in (*smalls, local):
+        copy.start()
     for g in visits:
         pltpu.make_async_copy(
             jac.at[lat, g, xi], jrecv.at[g, pl.ds(0, slots)], j_recv.at[g, 0]
@@ -137,20 +145,24 @@
         hrecv[0] = jnp.zeros(hrecv.shape[1:], hrecv.dtype)
         hrecv[2] = jnp.zeros(hrecv.shape[1:], hrecv.dtype)
 
+    for copy in smalls:
+        copy.wait()
     innov[...] = innov_ref[...].astype(jnp.float32)
     rinv[...] = rinv_ref[...].astype(jnp.float32)
+    cell = cell_ref[...].astype(jnp.float32)
+    live = cell >= 0.0
+    row = jnp.floor((cell + 0.5) * (1.0 / (cols + 1)))
+    rowcol[0] = jnp.where(live, row, AWAY)
+    rowcol[1] = jnp.where(live, cell - row * (cols + 1), AWAY)
 
     def build(i, carry):
         to_lat, to_x, _ = mate(i)
         for g in range(line):
             owner = to_lat * lon_n + g * inner + to_x
-            cell = cell_ref[owner].astype(jnp.float32)
-            live = cell >= 0.0
-            row = jnp.floor((cell + 0.5) * (1.0 / (cols + 1)))
             meta[i, g] = jnp.concatenate(
                 [
-                    jnp.where(live, row, AWAY),
-                    jnp.where(live, cell - row * (cols + 1), AWAY),
+                    rowcol[0, pl.ds(owner, 1), :],
+                    rowcol[1, pl.ds(owner, 1), :],
                     frac_ref[owner].astype(jnp.float32),
                     innov[pl.ds(owner, 1), :],
                     rinv[pl.ds(owner, 1), :],
@@ -187,9 +199,16 @@
         return carry
 
     half = plane // 2
-
-    def jac_landed(g, h):
-        landed(jrecv.at[g, pl.ds(h * half * slots, half * slots)], j_recv.at[g, h])
+    bounds = (0, half, plane - 1, plane)
+    moved_piece = 0 if moved < half else 1 if moved < plane - 1 else 2
+
+    def piece_of(i):
+        return (i >= half).astype(jnp.int32) + (i >= plane - 1).astype(jnp.int32)
+
+    def jac_landed(g, *which):
+        for h in which:
+            lanes = pl.ds(bounds[h] * slots, (bounds[h + 1] - bounds[h]) * slots)
+            landed(jrecv.at[g, lanes], j_recv.at[g, h])
 
     def send_jac(n):
         g = visits[n]
@@ -201,7 +220,7 @@
                 place = pl.ds(pl.multiple_of(i * slots, slots), slots)
                 remote(
                     jac.at[to_lat, g, to_x], jrecv.at[g, place], j_send,
-                    j_recv.at[g, i // half], at,
+                    j_recv.at[g, piece_of(i)], at,
                 ).start()
 
             return carry
@@ -290,8 +309,8 @@
     tiles = plane // tile
     pad = -(-(max(rows, cols) + 1) // 8) * 8
 
-    def terms(g, t, width):
-        lanes = pl.ds(pl.multiple_of(t * width, width), width)
+    def terms(g, start, width):
+        lanes = pl.ds(pl.multiple_of(start, slots), width)
         info = met[g, :, lanes].astype(jnp.float32)
         lat_w = weight_rows(info[0:1], info[2:3], pad)
         lon_w = weight_rows(info[1:2], info[3:4], pad)
@@ -319,7 +338,7 @@
         into = part.at[n]
 
         def one_tile(t, carry):
-            scaled, jac_t = terms(g, t, width)
+            scaled, jac_t = terms(g, t * width, width)
             into[...] += jnp.dot(scaled, jac_t, preferred_element_type=jnp.float32)
             return carry
 
@@ -392,15 +411,17 @@
                 field_landed(g, c)
 
         landed(tbl.at[g, rim], e_recv.at[g])
-        jac_landed(g, 1 - moved // half)
+        jac_landed(g, *(h for h in range(3) if h != moved_piece))
 
         @pl.when(lent_out(moved, g))
         def _():
-            landed(jrecv.at[g, pl.ds(slots, (half - 1) * slots)], j_recv.at[g, moved // half])
+            rest = bounds[moved_piece + 1] - bounds[moved_piece] - 1
+            if rest > 0:
+                landed(jrecv.at[g, pl.ds(0, rest * slots)], j_recv.at[g, moved_piece])
 
         @pl.when(jnp.logical_not(lent_out(moved, g)))
         def _():
-            jac_landed(g, moved // half)
+            jac_landed(g, moved_piece)
 
         compute(n, g)
         send_dep(g, 0, plane)
@@ -457,7 +478,7 @@
     def take_spare():
         landed(met.at[z, :, spare], l_recv)
         landed(jrecv.at[z, spare], s_recv)
-        return terms(z, plane, slots)
+        return terms(z, plane * slots, slots)
 
     def return_spare():
         to_lat, to_x = source(moved)
@@ -479,9 +500,8 @@
             scaled[:cells], jac_t, preferred_element_type=jnp.float32
         )
 
-    jac_landed(z, 0)
     if tiles > 1:
-        jac_landed(z, 1)
+        jac_landed(z, 0, 1, 2)
         compute(line - 1, z)
         send_dep(z, 0, plane)
 
@@ -494,6 +514,7 @@
         sums_landed(1, len(table_pieces))
         gmain[...] = part[line - 1, main, :] + arrived(main)
     else:
+        jac_landed(z, 0)
         scaled, jac_t = terms(z, 0, half * slots)
         part[line - 1] = jnp.dot(scaled, jac_t, preferred_element_type=jnp.float32)
         send_dep(z, 0, half)
@@ -501,13 +522,19 @@
 
         @pl.when(taker)
         def _():
-            add(terms(z, 1, half * slots))
+            jac_landed(z, 2)
+            add(terms(z, half * slots, half * slots))
             send_dep(z, half, plane)
             conclude(take_spare(), return_spare)
 
         @pl.when(jnp.logical_not(taker))
         def _():
-            conclude(terms(z, 1, half * slots), lambda: send_dep(z, half, plane))
+            add(terms(z, half * slots, (half - 1) * slots))
+            send_dep(z, half, plane - 1)
+            jac_landed(z, 2)
+            conclude(
+                terms(z, (plane - 1) * slots, slots), lambda: send_dep(z, plane - 1, plane)
+            )
 
     others = pl.ds(0, (plane - 1) * slots)
     for up in (False, True):
@@ -599,12 +626,17 @@
             pltpu.VMEM((3, rows, wide), bf16),
             pltpu.VMEM((lat_n, line, inner, 1, slots), f32),
         ),
-        in_specs=[anywhere, vmem, vmem, vmem, vmem, anywhere],
+        in_specs=[anywhere] * 6,
         out_specs=(vmem,) * 3,
         scratch_shapes=[
+            pltpu.VMEM((total, slots), jnp.int32),
+            pltpu.VMEM((total, 2, slots), bf16),
+            pltpu.VMEM((total, slots), bf16),
+            pltpu.VMEM((total, slots), bf16),
             pltpu.VMEM((rows, wide), bf16),
             pltpu.VMEM((total, slots), f32),
             pltpu.VMEM((total, slots), f32),
+            pltpu.VMEM((2, total, slots), f32),
             pltpu.VMEM((plane, line, 8, slots), bf16),
             pltpu.VMEM((8, slots), bf16),
             pltpu.VMEM((line, table, wide), bf16),
@@ -615,11 +647,11 @@
             pltpu.VMEM((line - 1, table, wide), bf16),
             pltpu.VMEM((line + 1, table, wide), bf16),
             pltpu.VMEM((table - cells, wide), bf16),
-            one, one, dma((line, 2)),
+            one, dma((4,)), one, dma((line, 2)),
             one, one, one, dma((line,)),
             one, one,
             one, one, one, one,
-            one, dma((line, 2)),
+            one, dma((line, 3)),
             one, one,
             one, dma((line + 1, 3)),
             one, one,
@@ -630,7 +662,7 @@
         ),
     )(
         field.reshape(cells, wide),
-        obs_cells,
+        obs_cells.reshape(total, slots),
         obs_frac.reshape(total, 2, slots),
         obs_innov.reshape(total, slots),
         obs_rinv.reshape(total, slots),

time: 47.5 us -> 46.9 us (0.987)
  Pallas kernels: 46.6 us -> 46.1 us
    pallas_call x1, Pallas kernels: 45.8 us -> 45.3 us  [shards(): pl.pallas_call(functools.partial(kernel, lat_n, lon_n, line, rows, cols,...]
where the time goes in v5:
time: 46.9 us; the launch traced here: 46.7 us
  Pallas kernels  46.1 us (98%)
  between operations  0.64 us (1%)
    pallas_call x1, Pallas kernels, shards(): pl.pallas_call(functools.partial(kernel, lat_n, lon_n, line, rows, cols,...  45.3 us

profile of v5, /device:TPU:0, one launch (start us, length us, event | category | flops | bytes accessed | tf_op | source)
XLA Modules:
  0.0 46.7 jit_solution(7462458264313466061)
XLA Ops:
  0.6 45.3 %shard_map.77 = (f32[256,384]{1,0:T(8,128)S(1)}, bf16[3,16,384]{2,1,0:T(8,128)(2,1)S(1)}, f32[4,4,2,1,128]{4,3,2,1,0:T(1,128)S(1)}) custom-call(bf16[256,384]{1,0:T(8,128)(2,1)} %bitcast.10, s32[32,128]{1,0:T(8,128)} %bitcast.11, bf16[32,2,128]{2,1,0:T(2,128)(2,1)} %bitcast.12, bf16[32,128]{1,0:T(8,128)(2,1)} %bitcast.13, bf16[32,128]{1,0:T(8,128)(2,1)} %bitcast.14, ...), custom_call_target="tpu_custom_call" | custom-call | tf_op jit(solution)/shard_map/pallas_call | solution.py:622
  45.9 0.8 %shard_map.78 = (f32[256,384]{1,0:T(8,128)}, f32[32,1,128]{2,1,0:T(1,128)}) custom-call(f32[256,384]{1,0:T(8,128)S(1)} %get-tuple-element.7.gmain, bf16[3,16,384]{2,1,0:T(8,128)(2,1)S(1)} %get-tuple-element.8.hrecv, f32[32,1,128]{2,1,0:T(1,128)S(1)} %bitcast.8), custom_call_target="tpu_custom_call" | custom-call | tf_op jit(solution)/shard_map/pallas_call | solution.py:671

commit v6 on v5

--- a/solution.py
+++ b/solution.py
@@ -133,12 +133,18 @@
 
     has_south, has_north = lat > 0, lat < lat_n - 1
     row_rim, edge_rim = pl.ds(cells, cols), pl.ds(halo, rows)
-    corner_rim, rim = pl.ds(halo + rows, rows), pl.ds(cells, cols + 2 * rows)
+    tip = min(8, rows)
+    corner_rim, rim = pl.ds(halo + rows, tip), pl.ds(cells, cols + 2 * rows)
+    sent_rim = pl.ds(cells, cols + rows + tip)
+    if rows > tip:
+        tbl[z, pl.ds(halo + rows + tip, rows - tip), :] = jnp.zeros(
+            (rows - tip, tbl.shape[2]), tbl.dtype
+        )
 
     @pl.when(jnp.logical_not(has_north))
     def _():
         tbl[z, row_rim, :] = jnp.zeros((cols, tbl.shape[2]), tbl.dtype)
-        tbl[z, corner_rim, :] = jnp.zeros((rows, tbl.shape[2]), tbl.dtype)
+        tbl[z, corner_rim, :] = jnp.zeros((tip, tbl.shape[2]), tbl.dtype)
 
     @pl.when(jnp.logical_not(has_south))
     def _():
@@ -232,7 +238,8 @@
 
         @pl.when(has_south)
         def _():
-            remote(edge, tbl.at[z_low, corner_rim], e_send, e_own, (lat_down, lon_down)).start()
+            remote(edge.at[pl.ds(0, tip)], tbl.at[z_low, corner_rim], e_send, e_own,
+                   (lat_down, lon_down)).start()
 
     early = plane - plane // 4
     lax.fori_loop(1, plane, send_meta, 0)
@@ -392,7 +399,7 @@
 
     @pl.when(has_north)
     def _():
-        landed(tbl.at[z, rim], e_own)
+        landed(tbl.at[z, sent_rim], e_own)
 
     @pl.when(jnp.logical_not(has_north))
     def _():
@@ -471,7 +478,7 @@
 
         @pl.when(has_north)
         def _():
-            remote(hsend.at[pl.ds(cols + rows, rows)], hrecv.at[2], h_send, h_recv,
+            remote(hsend.at[pl.ds(cols + rows, tip)], hrecv.at[2, pl.ds(0, tip)], h_send, h_recv,
                    (lat_up, lon_up)).start()
             remote(hsend.at[pl.ds(0, cols)], hrecv.at[0], h_send, h_recv, (lat_up, lon)).start()
 
@@ -546,7 +553,7 @@
                 landed(own_field, f_send)
     @pl.when(has_south)
     def _():
-        landed(tbl.at[z, rim], e_send)
+        landed(tbl.at[z, sent_rim], e_send)
 
     @pl.when(jnp.logical_not(has_south))
     def _():
@@ -573,7 +580,7 @@
     landed(gsend, g_send)
     @pl.when(has_north)
     def _():
-        landed(hsend, h_send)
+        landed(tbl.at[z, sent_rim], h_send)
 
     @pl.when(jnp.logical_not(has_north))
     def _():
@@ -581,7 +588,7 @@
 
     @pl.when(has_south)
     def _():
-        landed(hrecv, h_recv)
+        landed(tbl.at[z, sent_rim], h_recv)
 
     @pl.when(jnp.logical_not(has_south))
     def _():

time: 46.9 us -> 46.8 us (level)
  no operation moved by 1% of the time
where the time goes in v6:
time: 46.8 us; the launch traced here: 46.5 us
  Pallas kernels  45.9 us (98%)
  between operations  0.64 us (1%)
    pallas_call x1, Pallas kernels, shards(): pl.pallas_call(functools.partial(kernel, lat_n, lon_n, line, rows, cols,...  45.1 us

profile of v6, /device:TPU:0, one launch (start us, length us, event | category | flops | bytes accessed | tf_op | source)
XLA Modules:
  0.0 46.5 jit_solution(10242149793347333022)
XLA Ops:
  0.6 45.1 %shard_map.77 = (f32[256,384]{1,0:T(8,128)S(1)}, bf16[3,16,384]{2,1,0:T(8,128)(2,1)S(1)}, f32[4,4,2,1,128]{4,3,2,1,0:T(1,128)S(1)}) custom-call(bf16[256,384]{1,0:T(8,128)(2,1)} %bitcast.10, s32[32,128]{1,0:T(8,128)} %bitcast.11, bf16[32,2,128]{2,1,0:T(2,128)(2,1)} %bitcast.12, bf16[32,128]{1,0:T(8,128)(2,1)} %bitcast.13, bf16[32,128]{1,0:T(8,128)(2,1)} %bitcast.14, ...), custom_call_target="tpu_custom_call" | custom-call | tf_op jit(solution)/shard_map/pallas_call | solution.py:629
  45.7 0.8 %shard_map.78 = (f32[256,384]{1,0:T(8,128)}, f32[32,1,128]{2,1,0:T(1,128)}) custom-call(f32[256,384]{1,0:T(8,128)S(1)} %get-tuple-element.7.gmain, bf16[3,16,384]{2,1,0:T(8,128)(2,1)S(1)} %get-tuple-element.8.hrecv, f32[32,1,128]{2,1,0:T(1,128)S(1)} %bitcast.8), custom_call_target="tpu_custom_call" | custom-call | tf_op jit(solution)/shard_map/pallas_call | solution.py:678

commit v7 on v6

--- a/solution.py
+++ b/solution.py
@@ -471,9 +471,12 @@
             def _():
                 landed(rbuf.at[line, at], g_recv.at[line, c])
 
+    def gather_rim():
+        sums_landed(0, 1)
+        part[line - 1, rim, :] += arrived(rim)
+
     def send_rim(values):
-        sums_landed(0, 1)
-        hsend[...] = (values + arrived(rim)).astype(hsend.dtype)
+        hsend[...] = values.astype(hsend.dtype)
         remote(hsend.at[pl.ds(cols, rows)], hrecv.at[1], h_send, h_recv, (lat, lon_up)).start()
 
         @pl.when(has_north)
@@ -498,10 +501,10 @@
 
     def conclude(terms_of, send_rest):
         scaled, jac_t = terms_of
+        send_rest()
         send_rim(part[line - 1, rim, :] + jnp.dot(
             scaled[cells:], jac_t, preferred_element_type=jnp.float32
         ))
-        send_rest()
         sums_landed(1, len(table_pieces))
         gmain[...] = arrived(main) + part[line - 1, main, :] + jnp.dot(
             scaled[:cells], jac_t, preferred_element_type=jnp.float32
@@ -517,6 +520,7 @@
             add(take_spare())
             return_spare()
 
+        gather_rim()
         send_rim(part[line - 1, rim, :])
         sums_landed(1, len(table_pieces))
         gmain[...] = part[line - 1, main, :] + arrived(main)
@@ -531,12 +535,14 @@
         def _():
             jac_landed(z, 2)
             add(terms(z, half * slots, half * slots))
+            gather_rim()
             send_dep(z, half, plane)
             conclude(take_spare(), return_spare)
 
         @pl.when(jnp.logical_not(taker))
         def _():
             add(terms(z, half * slots, (half - 1) * slots))
+            gather_rim()
             send_dep(z, half, plane - 1)
             jac_landed(z, 2)
             conclude(

time: 46.8 us -> 46.8 us (level)
  no operation moved by 1% of the time
where the time goes in v7:
time: 46.8 us; the launch traced here: 46.5 us
  Pallas kernels  45.9 us (98%)
  between operations  0.64 us (1%)
    pallas_call x1, Pallas kernels, shards(): pl.pallas_call(functools.partial(kernel, lat_n, lon_n, line, rows, cols,...  45.1 us

profile of v7, /device:TPU:0, one launch (start us, length us, event | category | flops | bytes accessed | tf_op | source)
XLA Modules:
  0.0 46.5 jit_solution(7450810034013599668)
XLA Ops:
  0.6 45.1 %shard_map.77 = (f32[256,384]{1,0:T(8,128)S(1)}, bf16[3,16,384]{2,1,0:T(8,128)(2,1)S(1)}, f32[4,4,2,1,128]{4,3,2,1,0:T(1,128)S(1)}) custom-call(bf16[256,384]{1,0:T(8,128)(2,1)} %bitcast.10, s32[32,128]{1,0:T(8,128)} %bitcast.11, bf16[32,2,128]{2,1,0:T(2,128)(2,1)} %bitcast.12, bf16[32,128]{1,0:T(8,128)(2,1)} %bitcast.13, bf16[32,128]{1,0:T(8,128)(2,1)} %bitcast.14, ...), custom_call_target="tpu_custom_call" | custom-call | tf_op jit(solution)/shard_map/pallas_call | solution.py:635
  45.7 0.8 %shard_map.78 = (f32[256,384]{1,0:T(8,128)}, f32[32,1,128]{2,1,0:T(1,128)}) custom-call(f32[256,384]{1,0:T(8,128)S(1)} %get-tuple-element.7.gmain, bf16[3,16,384]{2,1,0:T(8,128)(2,1)S(1)} %get-tuple-element.8.hrecv, f32[32,1,128]{2,1,0:T(1,128)S(1)} %bitcast.8), custom_call_target="tpu_custom_call" | custom-call | tf_op jit(solution)/shard_map/pallas_call | solution.py:684

commit v8 on v7

--- a/solution.py
+++ b/solution.py
@@ -205,11 +205,12 @@
         return carry
 
     half = plane // 2
-    bounds = (0, half, plane - 1, plane)
-    moved_piece = 0 if moved < half else 1 if moved < plane - 1 else 2
+    tip_at = plane - 2
+    bounds = (0, half, tip_at, plane)
+    moved_piece = 0 if moved < half else 1 if moved < tip_at else 2
 
     def piece_of(i):
-        return (i >= half).astype(jnp.int32) + (i >= plane - 1).astype(jnp.int32)
+        return (i >= half).astype(jnp.int32) + (i >= tip_at).astype(jnp.int32)
 
     def jac_landed(g, *which):
         for h in which:
@@ -541,12 +542,12 @@
 
         @pl.when(jnp.logical_not(taker))
         def _():
-            add(terms(z, half * slots, (half - 1) * slots))
+            add(terms(z, half * slots, (tip_at - half) * slots))
             gather_rim()
-            send_dep(z, half, plane - 1)
+            send_dep(z, half, tip_at)
             jac_landed(z, 2)
             conclude(
-                terms(z, (plane - 1) * slots, slots), lambda: send_dep(z, plane - 1, plane)
+                terms(z, tip_at * slots, (plane - tip_at) * slots), lambda: send_dep(z, tip_at, plane)
             )
 
     others = pl.ds(0, (plane - 1) * slots)

time: 46.8 us -> 46.9 us (level)
  no operation moved by 1% of the time
where the time goes in v8:
time: 46.9 us; the launch traced here: 46.6 us
  Pallas kernels  46 us (98%)
  between operations  0.64 us (1%)
    pallas_call x1, Pallas kernels, shards(): pl.pallas_call(functools.partial(kernel, lat_n, lon_n, line, rows, cols,...  45.2 us

profile of v8, /device:TPU:0, one launch (start us, length us, event | category | flops | bytes accessed | tf_op | source)
XLA Modules:
  0.0 46.6 jit_solution(12089881549450913485)
XLA Ops:
  0.6 45.2 %shard_map.77 = (f32[256,384]{1,0:T(8,128)S(1)}, bf16[3,16,384]{2,1,0:T(8,128)(2,1)S(1)}, f32[4,4,2,1,128]{4,3,2,1,0:T(1,128)S(1)}) custom-call(bf16[256,384]{1,0:T(8,128)(2,1)} %bitcast.10, s32[32,128]{1,0:T(8,128)} %bitcast.11, bf16[32,2,128]{2,1,0:T(2,128)(2,1)} %bitcast.12, bf16[32,128]{1,0:T(8,128)(2,1)} %bitcast.13, bf16[32,128]{1,0:T(8,128)(2,1)} %bitcast.14, ...), custom_call_target="tpu_custom_call" | custom-call | tf_op jit(solution)/shard_map/pallas_call | solution.py:636
  45.8 0.8 %shard_map.78 = (f32[256,384]{1,0:T(8,128)}, f32[32,1,128]{2,1,0:T(1,128)}) custom-call(f32[256,384]{1,0:T(8,128)S(1)} %get-tuple-element.7.gmain, bf16[3,16,384]{2,1,0:T(8,128)(2,1)S(1)} %get-tuple-element.8.hrecv, f32[32,1,128]{2,1,0:T(1,128)S(1)} %bitcast.8), custom_call_target="tpu_custom_call" | custom-call | tf_op jit(solution)/shard_map/pallas_call | solution.py:685
